TPU v7x, 256 devices: a whole 4x4x8 slice. The times are simulated.
256 devices in a mesh: snap: 8 (over y, core), vtx: 32 (over z, x).
Axes of the slice: x: 4, y: 4, z: 8, core: 2. Of those that a mesh axis runs over, the one named last changes fastest.
Arguments:
- features: bfloat16 [16, 32768, 128], P('snap', 'vtx'), may hold values from -6 to 6
- tile_vals: bfloat16 [16, 256, 16, 128, 128], P('snap', 'vtx'), may hold values from -0.25 to 0.25
- tile_cols: int32 [16, 256, 16], P('snap', 'vtx'), may hold values from 0 to 255, as said below
- tile_count: int32 [16, 256], P('snap', 'vtx'), may hold values from 1 to 16
- gcn_weight: bfloat16 [128, 128], replicated, may hold values from -0.5 to 0.5
- gcn_bias: float32 [128], replicated, may hold values from -3 to 3
- input_weight: bfloat16 [128, 512], replicated, may hold values from -0.5 to 0.5
- recur_weight: bfloat16 [128, 512], replicated, may hold values from -0.5 to 0.5
- lstm_bias: float32 [512], replicated, may hold values from -4 to 4
- hidden_grad: bfloat16 [32, 1024, 16, 128], P('vtx', 'snap'), may hold values from -6 to 6
Outputs:
- hidden_states: bfloat16 [32, 1024, 16, 128], P('vtx', 'snap')
- grad_gcn_weight: float32 [128, 128], replicated
- grad_gcn_bias: float32 [128], replicated
- grad_input_weight: float32 [128, 512], replicated
- grad_recur_weight: float32 [128, 512], replicated
- grad_lstm_bias: float32 [512], replicated
Inputs may be any that keep to these rules, and one draw needn't show every extreme that they name: `tile_cols`: within one snapshot, the 16 slots of one row block name distinct column blocks, and all slots, live or not, of the row blocks j * 8 to (j + 1) * 8 - 1 together name at most one block of each group of 8 consecutive blocks.
All inputs are finite; a program needn't handle non-finite values.
Results may differ from a plain program's by a relative error of at most 0.0085.
Values may be sent and summed in bfloat16 or wider, within the bound.
No kernel may reach another device: no remote copies, remote signals or barrier semaphores. Data moves between devices by JAX's collectives and lax.ppermute only.
A program may use at most 128 MiB of HBM per device.

v0:
```python
import jax
import jax.numpy as jnp
from jax import lax
from jax.sharding import PartitionSpec as P


def silu_slope(grad_layer, pre_act):
    squeeze = jax.nn.sigmoid(pre_act)
    return (grad_layer.astype(jnp.float32) * squeeze * (1.0 + pre_act * (1.0 - squeeze))).astype(
        jnp.bfloat16
    )


def on_device(
    features,
    tile_vals,
    tile_cols,
    tile_count,
    gcn_weight,
    gcn_bias,
    input_weight,
    recur_weight,
    lstm_bias,
    hidden_grad,
):
    steps_dev, local_verts, feat_width = features.shape
    tile_size = tile_vals.shape[3]
    hidden_size = recur_weight.shape[0]
    live_mask = lax.broadcasted_iota(jnp.int32, tile_cols.shape, 2) < tile_count[:, :, None]
    snap_iota = lax.broadcasted_iota(jnp.int32, tile_cols.shape, 0)
    gathered = lax.all_gather(features, "vtx", axis=1, tiled=True)
    whole_blocks = gathered.reshape(steps_dev, -1, tile_size, feat_width)
    fetched_blocks = whole_blocks[snap_iota, tile_cols]
    blocks_used = jnp.where(
        live_mask[..., None, None], fetched_blocks, jnp.zeros_like(fetched_blocks)
    )
    summed = jnp.einsum(
        "svmij,svmjf->svif", tile_vals, blocks_used, preferred_element_type=jnp.float32
    )
    aggregated = summed.astype(jnp.bfloat16).reshape(steps_dev * local_verts, feat_width)
    pre_act = jnp.dot(aggregated, gcn_weight, preferred_element_type=jnp.float32) + gcn_bias
    layer_out = (
        jax.nn.silu(pre_act).astype(jnp.bfloat16).reshape(steps_dev, local_verts, feat_width)
    )
    vertex_inputs = lax.all_to_all(layer_out, "snap", split_axis=1, concat_axis=0, tiled=True)
    total_steps, vertex_rows, _ = vertex_inputs.shape
    flat_inputs = vertex_inputs.reshape(total_steps * vertex_rows, feat_width)
    input_gates = (
        jnp.dot(flat_inputs, input_weight, preferred_element_type=jnp.float32) + lstm_bias
    ).reshape(total_steps, vertex_rows, 4 * hidden_size)

    def advance(carried, gates_step):
        cell_state, last_out = carried
        pre_gates = gates_step + jnp.dot(last_out, recur_weight, preferred_element_type=jnp.float32)
        gate_in = jax.nn.sigmoid(pre_gates[:, :hidden_size])
        gate_keep = jax.nn.sigmoid(pre_gates[:, hidden_size : 2 * hidden_size])
        gate_new = jnp.tanh(pre_gates[:, 2 * hidden_size : 3 * hidden_size])
        gate_out = jax.nn.sigmoid(pre_gates[:, 3 * hidden_size :])
        cell_state = gate_keep * cell_state + gate_in * gate_new
        new_out = (gate_out * jnp.tanh(cell_state)).astype(jnp.bfloat16)
        return ((cell_state, new_out), (pre_gates, cell_state, new_out))

    zero_cell = jnp.zeros((vertex_rows, hidden_size), jnp.float32)
    start = (zero_cell, jnp.zeros((vertex_rows, hidden_size), jnp.bfloat16))
    _, (all_pre, all_cells, all_outs) = lax.scan(advance, start, input_gates)
    prev_cells = jnp.concatenate([zero_cell[None], all_cells[:-1]], axis=0)
    prev_outs = jnp.concatenate([start[1][None], all_outs[:-1]], axis=0)
    grad_outs = jnp.transpose(hidden_grad[0], (1, 0, 2)).astype(jnp.float32)

    def retreat(carried, step_items):
        grad_cell, grad_back = carried
        pre_gates, cell_state, prev_cell, grad_out = step_items
        gate_in = jax.nn.sigmoid(pre_gates[:, :hidden_size])
        gate_keep = jax.nn.sigmoid(pre_gates[:, hidden_size : 2 * hidden_size])
        gate_new = jnp.tanh(pre_gates[:, 2 * hidden_size : 3 * hidden_size])
        gate_out = jax.nn.sigmoid(pre_gates[:, 3 * hidden_size :])
        squash = jnp.tanh(cell_state)
        grad_total = grad_out + grad_back
        grad_cell = grad_cell + grad_total * gate_out * (1.0 - squash * squash)
        grad_gates = jnp.concatenate(
            [
                grad_cell * gate_new * gate_in * (1.0 - gate_in),
                grad_cell * prev_cell * gate_keep * (1.0 - gate_keep),
                grad_cell * gate_in * (1.0 - gate_new * gate_new),
                grad_total * squash * gate_out * (1.0 - gate_out),
            ],
            axis=1,
        ).astype(jnp.bfloat16)
        grad_back = jnp.einsum(
            "rg,hg->rh", grad_gates, recur_weight, preferred_element_type=jnp.float32
        )
        return ((grad_cell * gate_keep, grad_back), grad_gates)

    _, all_grad_gates = lax.scan(
        retreat, (zero_cell, zero_cell), (all_pre, all_cells, prev_cells, grad_outs), reverse=True
    )
    flat_gates = all_grad_gates.reshape(total_steps * vertex_rows, 4 * hidden_size)
    grad_input = jnp.einsum(
        "rf,rg->fg", flat_inputs, flat_gates, preferred_element_type=jnp.float32
    )
    grad_recur = jnp.einsum(
        "rh,rg->hg",
        prev_outs.reshape(total_steps * vertex_rows, hidden_size),
        flat_gates,
        preferred_element_type=jnp.float32,
    )
    grad_bias = jnp.sum(flat_gates.astype(jnp.float32), axis=0)
    grad_layer = jnp.einsum(
        "rg,fg->rf", flat_gates, input_weight, preferred_element_type=jnp.float32
    ).astype(jnp.bfloat16)
    grad_snap = lax.all_to_all(
        grad_layer.reshape(total_steps, vertex_rows, feat_width),
        "snap",
        split_axis=0,
        concat_axis=1,
        tiled=True,
    )
    grad_snap = grad_snap.reshape(steps_dev * local_verts, feat_width)
    grad_pre = silu_slope(grad_snap, pre_act)
    grad_gcn = jnp.einsum("rf,rg->fg", aggregated, grad_pre, preferred_element_type=jnp.float32)
    grad_gbias = jnp.sum(grad_pre.astype(jnp.float32), axis=0)
    grad_gcn, grad_gbias, grad_input, grad_recur, grad_bias = lax.psum(
        (grad_gcn, grad_gbias, grad_input, grad_recur, grad_bias), ("snap", "vtx")
    )
    hidden_states = jnp.transpose(all_outs, (1, 0, 2))[None]
    return (hidden_states, grad_gcn, grad_gbias, grad_input, grad_recur, grad_bias)


def solution(mesh):
    return jax.shard_map(
        on_device,
        mesh=mesh,
        in_specs=(
            P("snap", "vtx", None),
            P("snap", "vtx", None, None, None),
            P("snap", "vtx", None),
            P("snap", "vtx"),
            P(),
            P(),
            P(),
            P(),
            P(),
            P("vtx", "snap", None, None),
        ),
        out_specs=(P("vtx", "snap", None, None), P(), P(), P(), P(), P()),
        check_vma=False,
    )
```

profile of v0, /device:TPU:1, one launch (start us, length us, event | category | flops | bytes accessed | tf_op | source)
XLA Modules:
  0.0 570.2 jit_solution(6579747021246747212)
XLA Ops:
  9.5 145.1 %all-gather.2.cloned.1.call-done = bf16[2,32768,128]{2,1,0:T(8,128)(2,1)} async-done(((bf16[2,1024,128]{2,1,0:T(8,128)(2,1)}), bf16[2,32768,128]{2,1,0:T(8,128)(2,1)}) %all-gather.2.cloned.1.call-update) | async-done | bytes 16777232 | tf_op jit(solution)/shard_map/all_gather | solution.py:31
  154.6 15.9 %gather_fusion = bf16[256,128,128]{2,1,0:T(8,128)(2,1)} fusion(bf16[2,256,128,128]{3,2,1,0:T(8,128)(2,1)} %bitcast.136, s32[256]{0:T(256)S(1)} %reshape.144), kind=kCustom, calls=%fused_computation | custom fusion | bytes 16779264 | tf_op jit(solution)/shard_map/gather | solution.py:33
  170.4 8.2 %fusion.53 = bf16[2,8,128,128]{2,3,1,0:T(8,128)(2,1)S(1)} fusion(bf16[2,8,16,128,128]{4,3,2,1,0:T(8,128)(2,1)} %param.15, bf16[2,8,16,128,128]{4,3,2,1,0:T(8,128)(2,1)} %bitcast.132, pred[2,8,16]{2,1,0:T(8,128)(4,1)S(1)} %iota_compare_fusion), kind=kOutput, calls=%fused_computation.77 | convolution fusion | flops 1078198272 | bytes 17301760 | tf_op jit(solution)/shard_map/svmij,svmjf->svif/dot_general | solution.py:37
  179.4 1.4 multiply_convert_fusion.2
  180.8 1.3 copy.28
  182.2 5.3 all-to-all-start
  187.5 1.1 convert_bitcast_fusion.1
  188.6 8.3 %all-to-all-done = bf16[2,1024,128]{2,0,1:T(2,128)(2,1)S(1)} async-done(((bf16[2,1024,128]{2,0,1:T(2,128)(2,1)}), bf16[2,1024,128]{2,0,1:T(2,128)(2,1)S(1)}, u32[]{:S(2)}, u32[]{:S(2)}) %all-to-all-start) | async-done | bytes 524320 | tf_op jit(solution)/shard_map/all_to_all | solution.py:45
  197.1 2.6 convolution_add_fusion.1
  199.7 41.2 %while.38 = (s32[]{:T(128)}, f32[128,128]{1,0:T(8,128)S(1)}, bf16[128,128]{1,0:T(8,128)(2,1)S(1)}, f32[16,128,512]{2,1,0:T(8,128)}, f32[16,128,128]{2,1,0:T(8,12...) while((s32[]{:T(128)}, f32[128,128]{1,0:T(8,128)S(1)}, ...), condition=%wide.region_1.2_spmd.clone, body=%wide.region_0.1_spmd.clone.sunk | while | flops 17104900 | bytes 1541236 | solution.py:65
  199.7 1.9 bitcast_dynamic-update-slice_fusion.6
  202.3 1.8 bitcast_dynamic-update-slice_fusion.6
  204.9 1.9 bitcast_dynamic-update-slice_fusion.6
  207.5 1.8 bitcast_dynamic-update-slice_fusion.6
  210.0 1.8 bitcast_dynamic-update-slice_fusion.6
  212.6 1.8 bitcast_dynamic-update-slice_fusion.6
  215.2 1.8 bitcast_dynamic-update-slice_fusion.6
  217.7 1.8 bitcast_dynamic-update-slice_fusion.6
  220.3 1.9 bitcast_dynamic-update-slice_fusion.6
  222.9 1.8 bitcast_dynamic-update-slice_fusion.6
  225.5 1.8 bitcast_dynamic-update-slice_fusion.6
  228.0 1.8 bitcast_dynamic-update-slice_fusion.6
  230.6 1.8 bitcast_dynamic-update-slice_fusion.6
  233.2 1.8 bitcast_dynamic-update-slice_fusion.6
  235.7 1.9 bitcast_dynamic-update-slice_fusion.6
  238.3 1.9 bitcast_dynamic-update-slice_fusion.6
  241.0 1.3 concatenate.44
  242.5 49.4 %while.39 = (s32[]{:T(128)}, f32[128,128]{1,0:T(8,128)S(1)}, f32[128,128]{1,0:T(8,128)S(1)}, bf16[16,128,512]{2,1,0:T(8,128)(2,1)S(1)}, f32[16,128,128]{2,1,0:T(...) while((s32[]{:T(128)}, f32[128,128]{1,0:T(8,128)S(1)}, ...), condition=%wide.region_3.4_spmd.clone, body=%wide.region_2.3_spmd.clone.sunk | while | flops 18481156 | bytes 2162843 | solution.py:94
  242.5 1.0 dynamic-slice_bitcast_fusion.2
  245.6 1.0 dynamic-slice_bitcast_fusion.2
  248.7 1.0 dynamic-slice_bitcast_fusion.2
  251.8 1.0 dynamic-slice_bitcast_fusion.2
  254.8 1.0 dynamic-slice_bitcast_fusion.2
  264.1 1.0 dynamic-slice_bitcast_fusion.2
  273.4 1.0 dynamic-slice_bitcast_fusion.2
  291.9 2.1 copy.34
  294.0 1.5 convolution_convert_fusion
  295.5 4.3 all-to-all-start.1
  299.8 2.2 convolution_bitcast_fusion
  302.0 1.2 fusion.69
  303.1 6.1 %all-to-all-done.1 = bf16[16,128,128]{2,1,0:T(8,128)(2,1)S(1)} async-done(((bf16[16,128,128]{2,1,0:T(8,128)(2,1)}), bf16[16,128,128]{2,1,0:T(8,128)(2,1)S(1)}, u32[]{:S(2)}, u32[]{:S(2)}) %all-to-all-start.1) | async-done | bytes 524320 | tf_op jit(solution)/shard_map/all_to_all | solution.py:111
  309.5 1.0 copy-done.4
  312.0 1.1 copy.38
  313.4 73.9 %all-reduce.2 = (f32[128]{0:T(128)}, f32[512]{0:T(512)}) all-reduce(f32[128]{0:T(128)S(1)} %get-tuple-element.334, f32[512]{0:T(512)S(1)} %convert_reduce_fusion), channel_id=1, replica_groups=mesh['snap'=8,'vtx'=32] {'snap','vtx'}, use_global_device_ids=true, to_apply=%region_6.7 | all-reduce | flops 640 | bytes 5120 | tf_op jit(solution)/shard_map/psum | solution.py:122
  387.4 171.2 %all-reduce.6.cloned.1.call-done = (f32[128,128]{1,0:T(8,128)}, f32[128,512]{1,0:T(8,128)}, f32[128,512]{1,0:T(8,128)}) async-done(((f32[128,128]{1,0:T(8,128)}, f32[128,512]{1,0:T(8,128)}, f32[128,512]{1,0:T(8,128)}), (f32[128,128]{1,0:T(8,128)}, f32[128,512]{1,0:T(8,128)}, f32[128,512]{1,0:T(8,128)})) %all-reduce.6.cloned.1.call-update) | async-done | bytes 589840 | tf_op jit(solution)/shard_map/psum | solution.py:122
  558.6 1.5 copy.76
  560.0 1.7 copy.77
  561.7 1.7 copy.78
  (149 shorter events, 58.7 us)
Async XLA Ops:
  7.2 189.9 %copy-start = (bf16[128,512]{1,0:T(8,128)(2,1)S(1)}, bf16[128,512]{1,0:T(8,128)(2,1)}, u32[]{:S(2)}) copy-start(bf16[128,512]{1,0:T(8,128)(2,1)} %param.20) | copy-start | bytes 393220
  7.2 147.4 %all-gather.2.cloned.1.call-start = ((), (), s32[]{:S(2)}) async-start(), calls=%async_computation.2 | async-start | bytes 17301504 | tf_op jit(solution)/shard_map/all_gather | solution.py:31
  170.4 9.0 %copy-start.9 = (bf16[128,128]{1,0:T(8,128)(2,1)S(1)}, bf16[128,128]{1,0:T(8,128)(2,1)}, u32[]{:S(2)}) copy-start(bf16[128,128]{1,0:T(8,128)(2,1)} %param.18) | copy-start | bytes 98308
  170.4 9.0 %copy-start.10 = (f32[128]{0:T(128)S(1)}, f32[128]{0:T(128)}, u32[]{:S(2)}) copy-start(f32[128]{0:T(128)} %param.19) | copy-start | bytes 1540
  178.6 0.8 copy-start.6
  178.6 8.9 %copy-start.5 = (bf16[1,128,16,128]{3,2,1,0:T(8,128)(2,1)S(1)}, bf16[1,128,16,128]{3,2,1,0:T(8,128)(2,1)}, u32[]{:S(2)}) copy-start(bf16[1,128,16,128]{3,2,1,0:T(8,128)(2,1)} %param.23) | copy-start | bytes 1572868
  180.8 16.3 %copy-start.8 = (f32[512]{0:T(512)S(1)}, f32[512]{0:T(512)}, u32[]{:S(2)}) copy-start(f32[512]{0:T(512)} %param.22) | copy-start | bytes 6148
  182.2 14.8 %all-to-all-start = ((bf16[2,1024,128]{2,0,1:T(2,128)(2,1)}), bf16[2,1024,128]{2,0,1:T(2,128)(2,1)S(1)}, u32[]{:S(2)}, u32[]{:S(2)}) async-start(bf16[2,1024,128]{2,0,1:T(2,128)(2,1)} %copy.28), calls=%async_computation | async-start | bytes 1048576 | tf_op jit(solution)/shard_map/all_to_all | solution.py:45
  187.5 12.2 %copy-start.1 = (bf16[128,512]{1,0:T(8,128)(2,1)S(1)}, bf16[128,512]{1,0:T(8,128)(2,1)}, u32[]{:S(2)}) copy-start(bf16[128,512]{1,0:T(8,128)(2,1)} %param.21) | copy-start | bytes 393220
  240.9 1.3 copy-start.3
  295.5 13.8 %all-to-all-start.1 = ((bf16[16,128,128]{2,1,0:T(8,128)(2,1)}), bf16[16,128,128]{2,1,0:T(8,128)(2,1)S(1)}, u32[]{:S(2)}, u32[]{:S(2)}) async-start(bf16[16,128,128]{2,1,0:T(8,128)(2,1)} %bitcast.143), calls=%async_computation.1 | async-start | bytes 1048576 | tf_op jit(solution)/shard_map/all_to_all | solution.py:111
  299.8 258.8 %all-reduce.6.cloned.1.call-start = ((), (), s32[]{:S(2)}) async-start(), calls=%async_computation.3 | async-start | bytes 1179648 | tf_op jit(solution)/shard_map/psum | solution.py:122
  303.1 8.8 %copy-start.2 = (bf16[16,128,128]{2,1,0:T(8,128)(2,1)S(1)}, bf16[16,128,128]{2,1,0:T(8,128)(2,1)}, u32[]{:S(2)}) copy-start(bf16[16,128,128]{2,1,0:T(8,128)(2,1)} %get-tuple-element.229) | copy-start | bytes 1572868
  309.3 1.2 copy-start.4
  309.3 1.7 copy-start.7
Sparse Core Ops, SparseCore 0:
  10.6 143.9 all-gather.1
  312.1 246.4 all-reduce.5
where the time goes:
time: 573 us; the launch traced here: 570 us
  waiting for transfers between devices  331 us (58%)
  blocking collectives  73.9 us (13%)
  matrix products  50.5 us (9%)
  other arithmetic  44.9 us (8%)
  local copies, waits for them, and re-layouts  44.5 us (8%)
  between operations  14.2 us (2%)
  starting transfers between devices  9.64 us (2%)
    psum x1, waiting for transfers between devices, on_device(): lax.psum((grad_gcn, grad_gbias, grad_input, grad_recur, grad_bias), ('sna...  171 us
    all_gather x1, waiting for transfers between devices, on_device(): gathered = lax.all_gather(features, 'vtx', axis=1, tiled=True)  145 us
    psum x1, blocking collectives, on_device(): lax.psum((grad_gcn, grad_gbias, grad_input, grad_recur, grad_bias), ('sna...  73.9 us
    another operation x32, other arithmetic  29.8 us
    dot_general x16, matrix products, advance(): jnp.dot(last_out, recur_weight, preferred_element_type=jnp.float32)  29.5 us
    gather x1, local copies, waits for them, and re-layouts, on_device(): fetched_blocks = whole_blocks[snap_iota, tile_cols]  15.9 us
    squeeze x16, local copies, waits for them, and re-layouts, on_device(): _, (all_pre, all_cells, all_outs) = lax.scan(advance, start, input_gates)  15.6 us
  transfers between devices with their start and end apart: 4, of which 4 were waited for; matrix products, arithmetic and copies ran while one was open for 1% of the time, Pallas kernels for 0%

commit v1 on v0

v1 whole, which is shorter than its diff:
```python
import jax
import jax.numpy as jnp
from jax import lax
from jax.experimental import pallas as pl
from jax.experimental.pallas import tpu as pltpu
from jax.sharding import PartitionSpec as P

BF16 = jnp.bfloat16
F32 = jnp.float32
MIB = 1024 * 1024


def sigmoid(value):
    return 0.5 * jnp.tanh(0.5 * value) + 0.5


def pack_blocks(want_ref, feat_ref, send_ref, sems):
    peers, steps = send_ref.shape[:2]
    per_peer = feat_ref.shape[1]
    copies = []
    for peer in range(peers):
        for step in range(steps):
            pick = jnp.clip(want_ref[peer, step], 0, per_peer - 1)
            copy = pltpu.make_async_copy(
                feat_ref.at[step, pick], send_ref.at[peer, step], sems.at[peer, step]
            )
            copy.start()
            copies.append(copy)
    for copy in copies:
        copy.wait()


def aggregate(cols_ref, count_ref, recv_ref, tile_ref, out_ref, *, per_peer, group):
    step, block = pl.program_id(0), pl.program_id(1)
    peers = recv_ref.shape[0]
    slots, size, width = tile_ref.shape[2], tile_ref.shape[4], recv_ref.shape[3]
    live = count_ref[step, block]

    def add_group(at, total):
        tiles, blocks = [], []
        for inner in range(group):
            slot = at * group + inner
            peer = jnp.clip(cols_ref[step, block, slot] // per_peer, 0, peers - 1)
            held = recv_ref[peer, step].astype(F32)
            tiles.append(tile_ref[0, 0, slot])
            blocks.append(jnp.where(slot < live, held, 0.0).astype(BF16))
        return total + jnp.dot(
            jnp.concatenate(tiles, axis=1),
            jnp.concatenate(blocks, axis=0),
            preferred_element_type=F32,
        )

    groups = jnp.clip((live + group - 1) // group, 0, slots // group)
    total = lax.fori_loop(0, groups, add_group, jnp.zeros((size, width), F32))
    out_ref[0, 0] = total.astype(BF16)


def recur(
    agg_ref,
    hgrad_ref,
    gcn_w_ref,
    gcn_b_ref,
    w_ref,
    bias_ref,
    w_back_ref,
    out_ref,
    grads_ref,
    layer_s,
    slope_s,
    gates_s,
    cell_s,
    squash_s,
    hprev_s,
    dgates_s,
    dpre_s,
):
    steps, rows, width = agg_ref.shape
    hid = width

    def layer(t, _):
        pre = jnp.dot(agg_ref[t], gcn_w_ref[...], preferred_element_type=F32) + gcn_b_ref[...]
        squeeze = sigmoid(pre)
        layer_s[t] = (pre * squeeze).astype(BF16)
        slope_s[t] = squeeze * (1.0 + pre * (1.0 - squeeze))
        return 0

    lax.fori_loop(0, steps, layer, 0)

    hprev_s[0] = jnp.zeros((rows, hid), BF16)
    cell_s[0] = jnp.zeros((rows, hid), F32)

    def advance(t, _):
        both = jnp.concatenate([layer_s[t], hprev_s[t]], axis=1)
        pre = jnp.dot(both, w_ref[...], preferred_element_type=F32) + bias_ref[...]
        gate_in = sigmoid(pre[:, :hid])
        gate_keep = sigmoid(pre[:, hid : 2 * hid])
        gate_new = jnp.tanh(pre[:, 2 * hid : 3 * hid])
        gate_out = sigmoid(pre[:, 3 * hid :])
        cell = gate_keep * cell_s[t] + gate_in * gate_new
        squash = jnp.tanh(cell)
        out = (gate_out * squash).astype(BF16)
        gates_s[t, :, :hid] = gate_in
        gates_s[t, :, hid : 2 * hid] = gate_keep
        gates_s[t, :, 2 * hid : 3 * hid] = gate_new
        gates_s[t, :, 3 * hid :] = gate_out
        cell_s[t + 1] = cell
        squash_s[t] = squash
        hprev_s[t + 1] = out
        out_ref[t] = out
        return 0

    lax.fori_loop(0, steps, advance, 0)

    def retreat(k, carried):
        grad_cell, grad_back = carried
        t = steps - 1 - k
        gate_in = gates_s[t, :, :hid]
        gate_keep = gates_s[t, :, hid : 2 * hid]
        gate_new = gates_s[t, :, 2 * hid : 3 * hid]
        gate_out = gates_s[t, :, 3 * hid :]
        squash = squash_s[t]
        grad_total = hgrad_ref[t].astype(F32) + grad_back
        grad_cell = grad_cell + grad_total * gate_out * (1.0 - squash * squash)
        dgates = jnp.concatenate(
            [
                (grad_cell * gate_new * gate_in * (1.0 - gate_in)).astype(BF16),
                (grad_cell * cell_s[t] * gate_keep * (1.0 - gate_keep)).astype(BF16),
                (grad_cell * gate_in * (1.0 - gate_new * gate_new)).astype(BF16),
                (grad_total * squash * gate_out * (1.0 - gate_out)).astype(BF16),
            ],
            axis=1,
        )
        dgates_s[t] = dgates
        back = jnp.dot(dgates, w_back_ref[...], preferred_element_type=F32)
        grad_layer = back[:, :width].astype(BF16).astype(F32)
        dpre_s[t] = (grad_layer * slope_s[t]).astype(BF16)
        return grad_cell * gate_keep, back[:, width:]

    zero = jnp.zeros((rows, hid), F32)
    lax.fori_loop(0, steps, retreat, (zero, zero))

    flat_dgates = dgates_s[...].reshape(steps * rows, 4 * hid)
    flat_dpre = dpre_s[...].reshape(steps * rows, width)

    def over_rows(left, right):
        return lax.dot_general(
            left, right, (((0,), (0,)), ((), ())), preferred_element_type=F32
        )

    ones = jnp.ones((8, steps * rows), BF16)
    grads_ref[:width, : 4 * hid] = over_rows(
        layer_s[...].reshape(steps * rows, width), flat_dgates
    )
    grads_ref[width:, : 4 * hid] = over_rows(
        hprev_s[:steps].reshape(steps * rows, hid), flat_dgates
    )
    grads_ref[:width, 4 * hid :] = over_rows(
        agg_ref[...].reshape(steps * rows, width), flat_dpre
    )
    grads_ref[width:, 4 * hid :] = jnp.zeros((hid, width), F32)
    grad_bias = jnp.dot(ones, flat_dgates, preferred_element_type=F32)
    grad_gbias = jnp.dot(ones, flat_dpre, preferred_element_type=F32)
    for k in range(4):
        grads_ref[width + k : width + k + 1, 4 * hid :] = grad_bias[:1, k * hid : (k + 1) * hid]
    grads_ref[width + 4 : width + 5, 4 * hid :] = grad_gbias[:1]


def on_device(
    features,
    tile_vals,
    tile_cols,
    tile_count,
    gcn_weight,
    gcn_bias,
    input_weight,
    recur_weight,
    lstm_bias,
    hidden_grad,
):
    steps_dev, local_verts, width = features.shape
    blocks, slots, size = tile_vals.shape[1:4]
    hid = recur_weight.shape[0]
    n_vtx, n_snap = lax.axis_size("vtx"), lax.axis_size("snap")
    steps, rows = steps_dev * n_snap, local_verts // n_snap
    smem = pl.BlockSpec(memory_space=pltpu.SMEM)
    vmem = pl.BlockSpec(memory_space=pltpu.VMEM)

    with jax.named_scope("requests"):
        flat_cols = tile_cols.reshape(steps_dev, blocks * slots)
        peer_iota = lax.broadcasted_iota(jnp.int32, (n_vtx, steps_dev, blocks * slots), 0)
        named = (flat_cols // blocks)[None] == peer_iota
        need = jnp.max(jnp.where(named, (flat_cols % blocks)[None], 0), axis=2)
        need = jnp.pad(need, ((0, 0), (0, 128 - steps_dev)))
        want = lax.all_to_all(need, "vtx", 0, 0, tiled=True)

    with jax.named_scope("feature_blocks"):
        send = pl.pallas_call(
            pack_blocks,
            out_shape=jax.ShapeDtypeStruct((n_vtx, steps_dev, size, width), BF16),
            in_specs=[smem, vmem],
            out_specs=pl.BlockSpec(memory_space=pl.ANY),
            scratch_shapes=[pltpu.SemaphoreType.DMA((n_vtx, steps_dev))],
            name="pack_blocks",
        )(want, features.reshape(steps_dev, blocks, size, width))
        recv = lax.all_to_all(send, "vtx", 0, 0, tiled=True)

    with jax.named_scope("aggregate"):
        aggregated = pl.pallas_call(
            lambda *refs: aggregate(*refs, per_peer=blocks, group=4),
            out_shape=jax.ShapeDtypeStruct((blocks, steps_dev, size, width), BF16),
            grid=(steps_dev, blocks),
            in_specs=[
                smem,
                smem,
                vmem,
                pl.BlockSpec((1, 1, slots, size, size), lambda s, r: (s, r, 0, 0, 0)),
            ],
            out_specs=pl.BlockSpec((1, 1, size, width), lambda s, r: (r, s, 0, 0)),
            name="aggregate",
        )(tile_cols, tile_count, recv, tile_vals)

    with jax.named_scope("to_vertices"):
        by_step = lax.all_to_all(
            aggregated.reshape(n_snap, steps_dev, rows, width), "snap", 0, 0, tiled=True
        ).reshape(steps, rows, width)

    with jax.named_scope("recurrence"):
        outs, grads = pl.pallas_call(
            recur,
            out_shape=(
                jax.ShapeDtypeStruct((steps, rows, hid), BF16),
                jax.ShapeDtypeStruct((width + hid, 4 * hid + width), F32),
            ),
            in_specs=[vmem] * 7,
            out_specs=(vmem, vmem),
            scratch_shapes=[
                pltpu.VMEM((steps, rows, width), BF16),
                pltpu.VMEM((steps, rows, width), F32),
                pltpu.VMEM((steps, rows, 4 * hid), F32),
                pltpu.VMEM((steps + 1, rows, hid), F32),
                pltpu.VMEM((steps, rows, hid), F32),
                pltpu.VMEM((steps + 1, rows, hid), BF16),
                pltpu.VMEM((steps, rows, 4 * hid), BF16),
                pltpu.VMEM((steps, rows, width), BF16),
            ],
            compiler_params=pltpu.CompilerParams(vmem_limit_bytes=40 * MIB),
            name="recurrence",
        )(
            by_step,
            jnp.transpose(hidden_grad[0], (1, 0, 2)),
            gcn_weight,
            gcn_bias[None],
            jnp.concatenate([input_weight, recur_weight], axis=0),
            lstm_bias[None],
            jnp.concatenate([input_weight.T, recur_weight.T], axis=1),
        )

    with jax.named_scope("gradient_sums"):
        lanes = grads.shape[1]
        part = lax.all_to_all(grads.reshape(n_snap, n_vtx, lanes), "snap", 0, 0, tiled=True)
        part = lax.all_to_all(jnp.sum(part, axis=0), "vtx", 0, 0, tiled=True)
        part = jnp.broadcast_to(jnp.sum(part, axis=0, keepdims=True), (n_vtx, lanes))
        part = lax.all_to_all(part, "vtx", 0, 0, tiled=True)
        part = jnp.broadcast_to(part[None], (n_snap, n_vtx, lanes))
        total = lax.all_to_all(part, "snap", 0, 0, tiled=True).reshape(n_snap * n_vtx, lanes)

    hidden_states = jnp.transpose(outs, (1, 0, 2))[None]
    return (
        hidden_states,
        total[:width, 4 * hid :],
        total[width + 4, 4 * hid :],
        total[:width, : 4 * hid],
        total[width:, : 4 * hid],
        total[width : width + 4, 4 * hid :].reshape(4 * hid),
    )


def solution(mesh):
    return jax.shard_map(
        on_device,
        mesh=mesh,
        in_specs=(
            P("snap", "vtx", None),
            P("snap", "vtx", None, None, None),
            P("snap", "vtx", None),
            P("snap", "vtx"),
            P(),
            P(),
            P(),
            P(),
            P(),
            P("vtx", "snap", None, None),
        ),
        out_specs=(P("vtx", "snap", None, None), P(), P(), P(), P(), P()),
        check_vma=False,
    )
```

time: 573 us -> 184 us (0.32)
  waiting for transfers between devices: 331 us -> 18.8 us
  matrix products: 50.5 us -> 0 us
  other arithmetic: 44.9 us -> 0.28 us
  blocking collectives: 73.9 us -> 113 us
  local copies, waits for them, and re-layouts: 44.5 us -> 5.95 us
  Pallas kernels: 0 us -> 28.3 us
  between operations: 14.2 us -> 0.75 us
  starting transfers between devices: 9.64 us -> 16 us
    psum x1 -> x0, waiting for transfers between devices: 171 us -> none  [on_device(): lax.psum((grad_gcn, grad_gbias, grad_input, grad_recur, grad_bias), ('sna...]
    all_gather x1 -> x0, waiting for transfers between devices: 145 us -> none  [on_device(): gathered = lax.all_gather(features, 'vtx', axis=1, tiled=True)]
    all_to_all x0 -> x5, blocking collectives: none -> 113 us  [the longest x1 52 us: on_device(): recv = lax.all_to_all(send, 'vtx', 0, 0, tiled=True)]
    psum x1 -> x0, blocking collectives: 73.9 us -> none  [on_device(): lax.psum((grad_gcn, grad_gbias, grad_input, grad_recur, grad_bias), ('sna...]
    dot_general x39 -> x0, matrix products: 50.5 us -> none  [the longest x16 29.5 us: advance(): jnp.dot(last_out, recur_weight, preferred_element_type=jnp.float32)]
    another operation x32 -> x0, other arithmetic: 29.8 us -> none
    pallas_call x0 -> x3, Pallas kernels: none -> 28.3 us  [the longest x1 14.5 us: on_device(): pl.pallas_call(lambda *refs: aggregate(*refs, per_peer=blocks, group=4),...]
    gather x1 -> x0, local copies, waits for them, and re-layouts: 15.9 us -> none  [on_device(): fetched_blocks = whole_blocks[snap_iota, tile_cols]]
  transfers between devices with their start and end apart: 4 -> 2, of which waited for: 4 -> 2; matrix products, arithmetic and copies ran while one was open for 1% -> 1% of each run, Pallas kernels for 0% -> 0%
where the time goes in v1:
time: 184 us; the launch traced here: 183 us
  blocking collectives  113 us (61%)
  Pallas kernels  28.3 us (15%)
  waiting for transfers between devices  18.8 us (10%)
  starting transfers between devices  16 us (9%)
  local copies, waits for them, and re-layouts  5.95 us (3%)
    all_to_all x1, blocking collectives, on_device(): recv = lax.all_to_all(send, 'vtx', 0, 0, tiled=True)  52 us
    all_to_all x1, blocking collectives, on_device(): want = lax.all_to_all(need, 'vtx', 0, 0, tiled=True)  20.2 us
    all_to_all x1, blocking collectives, on_device(): part = lax.all_to_all(jnp.sum(part, axis=0), 'vtx', 0, 0, tiled=True)  14.8 us
    pallas_call x1, Pallas kernels, on_device(): pl.pallas_call(lambda *refs: aggregate(*refs, per_peer=blocks, group=4),...  14.5 us
    all_to_all x1, blocking collectives, on_device(): lax.all_to_all(grads.reshape(n_snap, n_vtx, lanes), 'snap', 0, 0, tiled=T...  14.2 us
    all_to_all x1, blocking collectives, on_device(): part = lax.all_to_all(part, 'vtx', 0, 0, tiled=True)  12.1 us
    pallas_call x1, Pallas kernels, on_device(): pl.pallas_call(recur, out_shape=(jax.ShapeDtypeStruct((steps, rows, hid),...  10.8 us
    all_to_all x1, waiting for transfers between devices, on_device(): lax.all_to_all(part, 'snap', 0, 0, tiled=True)  9.77 us
  transfers between devices with their start and end apart: 2, of which 2 were waited for; matrix products, arithmetic and copies ran while one was open for 1% of the time, Pallas kernels for 0%

profile of v1, /device:TPU:1, one launch (start us, length us, event | category | flops | bytes accessed | tf_op | source)
XLA Modules:
  0.0 183.4 jit_solution(5925385173556125690)
XLA Ops:
  0.6 0.8 reshape.91
  1.4 0.1 select_reduce_fusion
  1.6 0.1 copy.24
  1.6 20.2 %all_to_all.46 = s32[32,1,128]{2,1,0:T(1,128)} all-to-all(s32[32,1,128]{2,1,0:T(1,128)S(1)} %copy.24), channel_id=1, replica_groups=mesh['snap'=8,'vtx'=32] {'vtx'}, dimensions={0} | all-to-all | bytes 32768 | tf_op jit(solution)/shard_map/requests/all_to_all | solution.py:194
  21.8 3.0 %pack_blocks.1 = bf16[32,2,128,128]{3,2,1,0:T(8,128)(2,1)} custom-call(s32[32,128]{1,0:T(8,128)} %bitcast.40, bf16[2,8,128,128]{3,2,1,0:T(8,128)(2,1)} %bitcast.36), custom_call_target="tpu_custom_call" | custom-call | tf_op jit(solution)/shard_map/feature_blocks/pack_blocks/pallas_call | solution.py:197
  24.8 52.0 %all_to_all.47.refs_2_ = bf16[32,2,128,128]{3,2,1,0:T(8,128)(2,1)} all-to-all(bf16[32,2,128,128]{3,2,1,0:T(8,128)(2,1)} %pack_blocks.1), channel_id=1, replica_groups=mesh['snap'=8,'vtx'=32] {'vtx'}, dimensions={0} | all-to-all | bytes 4194304 | tf_op jit(solution)/shard_map/feature_blocks/all_to_all | solution.py:205
  76.8 0.0 copy-start.3
  76.8 14.5 %aggregate.1 = bf16[8,2,128,128]{3,2,1,0:T(8,128)(2,1)} custom-call(s32[2,8,16]{2,1,0:T(8,128)} %refs_0_.1, s32[2,8]{1,0:T(2,128)} %refs_1_.1, bf16[32,2,128,128]{3,2,1,0:T(8,128)(2,1)} %all_to_all.47.refs_2_, bf16[2,8,16,128,128]{4,3,2,1,0:T(8,128)(2,1)} %refs_3_.1), custom_call_target="tpu_custom_call" | custom-call | tf_op jit(solution)/shard_map/aggregate/aggregate/pallas_call | solution.py:208
  91.4 0.0 copy-start.5
  91.4 0.0 copy-start.4
  91.4 0.0 copy-start
  91.4 0.0 copy-start.1
  91.4 0.0 copy-start.2
  91.4 9.2 %all-to-all-start.2 = ((bf16[8,2,128,128]{3,2,1,0:T(8,128)(2,1)}), bf16[8,2,128,128]{3,2,1,0:T(8,128)(2,1)S(1)}, u32[]{:S(2)}, u32[]{:S(2)}) async-start(bf16[8,2,128,128]{3,2,1,0:T(8,128)(2,1)} %aggregate.1), calls=%async_computation.2 | async-start | bytes 1048576 | tf_op jit(solution)/shard_map/to_vertices/all_to_all | solution.py:223
  100.5 0.0 copy-done.3
  100.6 0.1 copy.32
  100.7 0.0 copy-done.5
  100.7 0.1 copy.26
  100.8 0.0 copy-done.4
  100.8 0.1 copy.27
  101.0 9.0 %all-to-all-done.2 = bf16[8,2,128,128]{3,2,1,0:T(8,128)(2,1)S(1)} async-done(((bf16[8,2,128,128]{3,2,1,0:T(8,128)(2,1)}), bf16[8,2,128,128]{3,2,1,0:T(8,128)(2,1)S(1)}, u32[]{:S(2)}, u32[]{:S(2)}) %all-to-all-start.2) | async-done | bytes 524320 | tf_op jit(solution)/shard_map/to_vertices/all_to_all | solution.py:223
  110.0 0.0 copy-done
  110.0 0.0 copy-done.1
  110.0 0.0 copy-done.2
  110.0 10.8 %recurrence.1 = (bf16[16,128,128]{2,1,0:T(8,128)(2,1)S(1)}, f32[256,640]{1,0:T(8,128)S(1)}) custom-call(bf16[16,128,128]{2,1,0:T(8,128)(2,1)S(1)} %bitcast.26, bf16[16,128,128]{2,1,0:T(8,128)(2,1)S(1)} %bitcast.27, bf16[128,128]{1,0:T(8,128)(2,1)S(1)} %copy-done, f32[1,128]{1,0:T(1,128)S(1)} %bitcast.31, bf16[256,512]{1,0:T(8,128)(2,1)S(1)} %pad_maximum_fusion.w_ref, ...), custom_call_target="tpu_custom_call" | custom-call | tf_op jit(solution)/shard_map/recurrence/recurrence/pallas_call | solution.py:228
  120.8 14.2 %all_to_all.48 = f32[8,32,640]{2,1,0:T(8,128)S(1)} all-to-all(f32[8,32,640]{2,1,0:T(8,128)S(1)} %bitcast.28), channel_id=1, replica_groups=mesh['snap'=8,'vtx'=32] {'snap'}, dimensions={0} | all-to-all | bytes 1310720 | tf_op jit(solution)/shard_map/gradient_sums/all_to_all | solution.py:260
  135.1 0.1 all_to_all.35
  135.1 14.8 %all_to_all.49 = f32[32,1,640]{2,1,0:T(1,128)S(1)} all-to-all(f32[32,1,640]{2,1,0:T(1,128)S(1)} %all_to_all.35), channel_id=1, replica_groups=mesh['snap'=8,'vtx'=32] {'vtx'}, dimensions={0} | all-to-all | bytes 163840 | tf_op jit(solution)/shard_map/gradient_sums/all_to_all | solution.py:261
  149.9 0.1 reduce_sum.19
  150.0 12.1 %all_to_all.50 = f32[32,1,640]{2,1,0:T(1,128)S(1)} all-to-all(f32[32,1,640]{2,1,0:T(1,128)S(1)} %broadcast_in_dim.42), channel_id=1, replica_groups=mesh['snap'=8,'vtx'=32] {'vtx'}, dimensions={0} | all-to-all | bytes 163840 | tf_op jit(solution)/shard_map/gradient_sums/all_to_all | solution.py:263
  162.2 0.9 broadcast_in_dim.44
  163.1 6.8 %all-to-all-start.6 = ((f32[8,32,640]{2,1,0:T(8,128)}), f32[8,32,640]{2,1,0:T(8,128)S(1)}, u32[]{:S(2)}, u32[]{:S(2)}) async-start(f32[8,32,640]{2,1,0:T(8,128)} %broadcast_in_dim.44), calls=%async_computation.6 | async-start | bytes 1310720 | tf_op jit(solution)/shard_map/gradient_sums/all_to_all | solution.py:265
  169.9 1.1 copy.28
  171.0 9.8 %all-to-all-done.6 = f32[8,32,640]{2,1,0:T(8,128)S(1)} async-done(((f32[8,32,640]{2,1,0:T(8,128)}), f32[8,32,640]{2,1,0:T(8,128)S(1)}, u32[]{:S(2)}, u32[]{:S(2)}) %all-to-all-start.6) | async-done | bytes 655392 | tf_op jit(solution)/shard_map/gradient_sums/all_to_all | solution.py:265
  180.8 0.9 fusion
  181.7 0.6 slice.20
  182.3 0.6 slice_bitcast_fusion
  182.9 0.5 slice_bitcast_fusion.1
  (7 shorter events, 0.2 us)
Async XLA Ops:
  76.8 23.7 %copy-start.3 = (bf16[1,128,16,128]{3,2,1,0:T(8,128)(2,1)S(1)}, bf16[1,128,16,128]{3,2,1,0:T(8,128)(2,1)}, u32[]{:S(2)}) copy-start(bf16[1,128,16,128]{3,2,1,0:T(8,128)(2,1)} %param.19) | copy-start | bytes 1572868
  91.4 9.3 %copy-start.5 = (bf16[128,512]{1,0:T(8,128)(2,1)S(1)}, bf16[128,512]{1,0:T(8,128)(2,1)}, u32[]{:S(2)}) copy-start(bf16[128,512]{1,0:T(8,128)(2,1)} %param.16) | copy-start | bytes 393220
  91.4 9.5 %copy-start.4 = (bf16[128,512]{1,0:T(8,128)(2,1)S(1)}, bf16[128,512]{1,0:T(8,128)(2,1)}, u32[]{:S(2)}) copy-start(bf16[128,512]{1,0:T(8,128)(2,1)} %param.17) | copy-start | bytes 393220
  91.4 18.7 %copy-start = (bf16[128,128]{1,0:T(8,128)(2,1)S(1)}, bf16[128,128]{1,0:T(8,128)(2,1)}, u32[]{:S(2)}) copy-start(bf16[128,128]{1,0:T(8,128)(2,1)} %gcn_w_ref.1) | copy-start | bytes 98308
  91.4 18.7 %copy-start.1 = (f32[512]{0:T(512)S(1)}, f32[512]{0:T(512)}, u32[]{:S(2)}) copy-start(f32[512]{0:T(512)} %param.18) | copy-start | bytes 6148
  91.4 18.7 %copy-start.2 = (f32[128]{0:T(128)S(1)}, f32[128]{0:T(128)}, u32[]{:S(2)}) copy-start(f32[128]{0:T(128)} %param.15) | copy-start | bytes 1540
  91.4 18.6 %all-to-all-start.2 = ((bf16[8,2,128,128]{3,2,1,0:T(8,128)(2,1)}), bf16[8,2,128,128]{3,2,1,0:T(8,128)(2,1)S(1)}, u32[]{:S(2)}, u32[]{:S(2)}) async-start(bf16[8,2,128,128]{3,2,1,0:T(8,128)(2,1)} %aggregate.1), calls=%async_computation.2 | async-start | bytes 1048576 | tf_op jit(solution)/shard_map/to_vertices/all_to_all | solution.py:223
  163.1 17.7 %all-to-all-start.6 = ((f32[8,32,640]{2,1,0:T(8,128)}), f32[8,32,640]{2,1,0:T(8,128)S(1)}, u32[]{:S(2)}, u32[]{:S(2)}) async-start(f32[8,32,640]{2,1,0:T(8,128)} %broadcast_in_dim.44), calls=%async_computation.6 | async-start | bytes 1310720 | tf_op jit(solution)/shard_map/gradient_sums/all_to_all | solution.py:265

commit v2 on v1

v2 whole, which is shorter than its diff:
```python
import functools

import jax
import jax.numpy as jnp
from jax import lax
from jax.experimental import pallas as pl
from jax.experimental.pallas import tpu as pltpu
from jax.sharding import Mesh
from jax.sharding import PartitionSpec as P

BF16 = jnp.bfloat16
F32 = jnp.float32
MIB = 1024 * 1024
LANES = 128
VTX, SNAP = ("z", "x"), ("y", "core")
SCATTER, ROUND = ("y", "x"), ("core", "z")


def sigmoid(value):
    return 0.5 * jnp.tanh(0.5 * value) + 0.5


def find_requests(cols_ref, feat_ref, need_ref, held_ref, sem, *, per_peer):
    copy = pltpu.make_async_copy(feat_ref, held_ref, sem)
    copy.start()
    steps, blocks, slots = cols_ref.shape
    peers = need_ref.shape[0]
    peer_iota = lax.broadcasted_iota(jnp.int32, (peers, slots), 0)
    lane = lax.broadcasted_iota(jnp.int32, need_ref.shape, 1)
    need = jnp.zeros(need_ref.shape, jnp.int32)
    for step in range(steps):
        found = jnp.zeros((peers, slots), jnp.int32)
        for block in range(blocks):
            cols = jnp.broadcast_to(cols_ref[step, block : block + 1, :], (peers, slots))
            inner = cols - peer_iota * per_peer
            found = jnp.maximum(found, jnp.where(inner < per_peer, inner, 0))
        need = jnp.where(lane == step, jnp.max(found, axis=1, keepdims=True), need)
    need_ref[...] = need
    copy.wait()


def pack_blocks(want_ref, feat_ref, send_ref):
    peers, steps = send_ref.shape[:2]
    per_peer = feat_ref.shape[1]

    def fill(peer, _):
        for step in range(steps):
            pick = jnp.clip(want_ref[peer, step], 0, per_peer - 1)
            send_ref[peer, step] = feat_ref[step, pick]
        return 0

    lax.fori_loop(0, peers, fill, 0, unroll=4)


def aggregate(cols_ref, count_ref, recv_ref, tile_ref, out_ref, held_tiles, sems, *, per_peer):
    steps, blocks, slots, size = tile_ref.shape[:4]
    peers, width = recv_ref.shape[0], recv_ref.shape[3]

    def fetch(step, block):
        return pltpu.make_async_copy(
            tile_ref.at[step, block], held_tiles.at[step, block], sems.at[step, block]
        )

    for block in range(blocks):
        for step in range(steps):
            fetch(step, block).start()

    def one_block(block, _):
        for step in range(steps):
            fetch(step, block).wait()
        for step in range(steps):
            live = count_ref[step, block]
            total = jnp.zeros((size, width), F32)
            for slot in range(0, slots, 2):
                tiles, held = [], []
                for at in (slot, slot + 1):
                    peer = jnp.clip(cols_ref[step, block, at] // per_peer, 0, peers - 1)
                    picked = recv_ref[peer, step]
                    tiles.append(held_tiles[step, block, at])
                    held.append(lax.select_n(at < live, jnp.zeros_like(picked), picked))
                total = total + jnp.dot(
                    jnp.concatenate(tiles, axis=1),
                    jnp.concatenate(held, axis=0),
                    preferred_element_type=F32,
                )
            out_ref[block, step] = total.astype(BF16)
        return 0

    lax.fori_loop(0, blocks, one_block, 0)


def recur(
    agg_ref,
    hgrad_ref,
    gcn_w_ref,
    gcn_b_ref,
    w_ref,
    bias_ref,
    w_back_ref,
    out_ref,
    grads_ref,
    layer_s,
    slope_s,
    gates_s,
    cell_s,
    squash_s,
    hprev_s,
    dgates_s,
    dpre_s,
):
    steps, rows, width = agg_ref.shape
    hid = width

    def layer(t, _):
        pre = jnp.dot(agg_ref[t], gcn_w_ref[...], preferred_element_type=F32) + gcn_b_ref[...]
        squeeze = sigmoid(pre)
        layer_s[t] = (pre * squeeze).astype(BF16)
        slope_s[t] = squeeze * (1.0 + pre * (1.0 - squeeze))
        return 0

    lax.fori_loop(0, steps, layer, 0)

    hprev_s[0] = jnp.zeros((rows, hid), BF16)
    cell_s[0] = jnp.zeros((rows, hid), F32)

    def advance(t, _):
        both = jnp.concatenate([layer_s[t], hprev_s[t]], axis=1)
        pre = jnp.dot(both, w_ref[...], preferred_element_type=F32) + bias_ref[...]
        gate_in = sigmoid(pre[:, :hid])
        gate_keep = sigmoid(pre[:, hid : 2 * hid])
        gate_new = jnp.tanh(pre[:, 2 * hid : 3 * hid])
        gate_out = sigmoid(pre[:, 3 * hid :])
        cell = gate_keep * cell_s[t] + gate_in * gate_new
        squash = jnp.tanh(cell)
        out = (gate_out * squash).astype(BF16)
        gates_s[t, :, :hid] = gate_in
        gates_s[t, :, hid : 2 * hid] = gate_keep
        gates_s[t, :, 2 * hid : 3 * hid] = gate_new
        gates_s[t, :, 3 * hid :] = gate_out
        cell_s[t + 1] = cell
        squash_s[t] = squash
        hprev_s[t + 1] = out
        out_ref[t] = out
        return 0

    lax.fori_loop(0, steps, advance, 0)

    def retreat(k, carried):
        grad_cell, grad_back = carried
        t = steps - 1 - k
        gate_in = gates_s[t, :, :hid]
        gate_keep = gates_s[t, :, hid : 2 * hid]
        gate_new = gates_s[t, :, 2 * hid : 3 * hid]
        gate_out = gates_s[t, :, 3 * hid :]
        squash = squash_s[t]
        grad_total = hgrad_ref[t].astype(F32) + grad_back
        grad_cell = grad_cell + grad_total * gate_out * (1.0 - squash * squash)
        dgates = jnp.concatenate(
            [
                (grad_cell * gate_new * gate_in * (1.0 - gate_in)).astype(BF16),
                (grad_cell * cell_s[t] * gate_keep * (1.0 - gate_keep)).astype(BF16),
                (grad_cell * gate_in * (1.0 - gate_new * gate_new)).astype(BF16),
                (grad_total * squash * gate_out * (1.0 - gate_out)).astype(BF16),
            ],
            axis=1,
        )
        dgates_s[t] = dgates
        back = jnp.dot(dgates, w_back_ref[...], preferred_element_type=F32)
        grad_layer = back[:, :width].astype(BF16).astype(F32)
        dpre_s[t] = (grad_layer * slope_s[t]).astype(BF16)
        return grad_cell * gate_keep, back[:, width:]

    zero = jnp.zeros((rows, hid), F32)
    lax.fori_loop(0, steps, retreat, (zero, zero))

    flat_dgates = dgates_s[...].reshape(steps * rows, 4 * hid)
    flat_dpre = dpre_s[...].reshape(steps * rows, width)

    def over_rows(left, right):
        return lax.dot_general(
            left, right, (((0,), (0,)), ((), ())), preferred_element_type=F32
        )

    def put(at, value):
        height = value.shape[0]
        for k in range(value.shape[1] // LANES):
            grads_ref[pl.ds(at + k * height, height), :] = value[
                :, k * LANES : (k + 1) * LANES
            ].astype(BF16)
        return at + value.shape[1] // LANES * height

    ones = jnp.ones((8, steps * rows), BF16)
    at = put(0, over_rows(layer_s[...].reshape(steps * rows, width), flat_dgates))
    at = put(at, over_rows(hprev_s[:steps].reshape(steps * rows, hid), flat_dgates))
    at = put(at, over_rows(agg_ref[...].reshape(steps * rows, width), flat_dpre))
    at = put(at, jnp.dot(ones, flat_dgates, preferred_element_type=F32))
    at = put(at, jnp.dot(ones, flat_dpre, preferred_element_type=F32))
    grads_ref[pl.ds(at, grads_ref.shape[0] - at), :] = jnp.zeros(
        (grads_ref.shape[0] - at, LANES), BF16
    )


def sum_parts(part_ref, out_ref):
    total = jnp.sum(part_ref[...].astype(F32), axis=0)
    out_ref[...] = jnp.broadcast_to(total.astype(out_ref.dtype)[None], out_ref.shape)


def unpack(total_ref, *out_refs):
    at = 0
    for out_ref in out_refs:
        height, columns = out_ref.shape
        taken = max(height, 8)
        for k in range(columns // LANES):
            out_ref[:, k * LANES : (k + 1) * LANES] = total_ref[pl.ds(at, taken), :].astype(F32)[
                :height
            ]
            at += taken


def on_device(
    features,
    tile_vals,
    tile_cols,
    tile_count,
    gcn_weight,
    gcn_bias,
    input_weight,
    recur_weight,
    lstm_bias,
    hidden_grad,
):
    steps_dev, local_verts, width = features.shape
    blocks, slots, size = tile_vals.shape[1:4]
    hid = recur_weight.shape[0]
    n_vtx, n_snap = lax.axis_size(VTX), lax.axis_size(SNAP)
    steps, rows = steps_dev * n_snap, local_verts // n_snap
    n_scatter, n_round = lax.axis_size(SCATTER), lax.axis_size(ROUND)
    held_rows = (2 * 4 * hid + width) * width // LANES + 8 * (4 * hid + width) // LANES
    share = -(-held_rows // (8 * n_scatter)) * 8
    grad_rows = n_scatter * share
    smem = pl.BlockSpec(memory_space=pltpu.SMEM)
    vmem = pl.BlockSpec(memory_space=pltpu.VMEM)
    hbm = pl.BlockSpec(memory_space=pltpu.HBM)

    with jax.named_scope("requests"):
        need, held_features = pl.pallas_call(
            functools.partial(find_requests, per_peer=blocks),
            out_shape=(
                jax.ShapeDtypeStruct((n_vtx, LANES), jnp.int32),
                jax.ShapeDtypeStruct((steps_dev, blocks, size, width), BF16),
            ),
            in_specs=[vmem, hbm],
            out_specs=(vmem, vmem),
            scratch_shapes=[pltpu.SemaphoreType.DMA],
            compiler_params=pltpu.CompilerParams(vmem_limit_bytes=8 * MIB),
            name="find_requests",
        )(tile_cols, features.reshape(steps_dev, blocks, size, width))
        want = lax.all_to_all(need, VTX, 0, 0, tiled=True)

    with jax.named_scope("feature_blocks"):
        send = pl.pallas_call(
            pack_blocks,
            out_shape=jax.ShapeDtypeStruct((n_vtx, steps_dev, size, width), BF16),
            in_specs=[smem, vmem],
            out_specs=vmem,
            compiler_params=pltpu.CompilerParams(vmem_limit_bytes=8 * MIB),
            name="pack_blocks",
        )(want, held_features)
        recv = lax.all_to_all(send, VTX, 0, 0, tiled=True)

    with jax.named_scope("aggregate"):
        aggregated = pl.pallas_call(
            functools.partial(aggregate, per_peer=blocks),
            out_shape=jax.ShapeDtypeStruct((blocks, steps_dev, size, width), BF16),
            in_specs=[smem, smem, vmem, hbm],
            out_specs=vmem,
            scratch_shapes=[
                pltpu.VMEM(tile_vals.shape, BF16),
                pltpu.SemaphoreType.DMA((steps_dev, blocks)),
            ],
            compiler_params=pltpu.CompilerParams(vmem_limit_bytes=50 * MIB),
            name="aggregate",
        )(tile_cols, tile_count, recv, tile_vals)

    with jax.named_scope("to_vertices"):
        by_step = lax.all_to_all(
            aggregated.reshape(n_snap, steps_dev, rows, width), SNAP, 0, 0, tiled=True
        ).reshape(steps, rows, width)

    with jax.named_scope("recurrence"):
        outs, grads = pl.pallas_call(
            recur,
            out_shape=(
                jax.ShapeDtypeStruct((steps, rows, hid), BF16),
                jax.ShapeDtypeStruct((grad_rows, LANES), BF16),
            ),
            in_specs=[vmem] * 7,
            out_specs=(vmem, vmem),
            scratch_shapes=[
                pltpu.VMEM((steps, rows, width), BF16),
                pltpu.VMEM((steps, rows, width), F32),
                pltpu.VMEM((steps, rows, 4 * hid), F32),
                pltpu.VMEM((steps + 1, rows, hid), F32),
                pltpu.VMEM((steps, rows, hid), F32),
                pltpu.VMEM((steps + 1, rows, hid), BF16),
                pltpu.VMEM((steps, rows, 4 * hid), BF16),
                pltpu.VMEM((steps, rows, width), BF16),
            ],
            compiler_params=pltpu.CompilerParams(vmem_limit_bytes=40 * MIB),
            name="recurrence",
        )(
            by_step,
            jnp.transpose(hidden_grad[0], (1, 0, 2)),
            gcn_weight,
            gcn_bias[None],
            jnp.concatenate([input_weight, recur_weight], axis=0),
            lstm_bias[None],
            jnp.concatenate([input_weight.T, recur_weight.T], axis=1),
        )

    with jax.named_scope("gradient_sums"):
        part = lax.all_to_all(
            grads.reshape(n_scatter, share, LANES), SCATTER, 0, 0, tiled=True
        )
        part = pl.pallas_call(
            sum_parts,
            out_shape=jax.ShapeDtypeStruct((n_round, share, LANES), BF16),
            in_specs=[vmem],
            out_specs=vmem,
            compiler_params=pltpu.CompilerParams(vmem_limit_bytes=8 * MIB),
            name="sum_scattered",
        )(part)
        part = lax.all_to_all(part, ROUND, 0, 0, tiled=True)
        part = pl.pallas_call(
            sum_parts,
            out_shape=jax.ShapeDtypeStruct((n_scatter, share, LANES), BF16),
            in_specs=[vmem],
            out_specs=vmem,
            compiler_params=pltpu.CompilerParams(vmem_limit_bytes=8 * MIB),
            name="sum_round",
        )(part)
        total = lax.all_to_all(part, SCATTER, 0, 0, tiled=True)
        grad_input, grad_recur, grad_gcn, grad_bias, grad_gbias = pl.pallas_call(
            unpack,
            out_shape=tuple(
                jax.ShapeDtypeStruct(shape, F32)
                for shape in (
                    (width, 4 * hid),
                    (hid, 4 * hid),
                    (width, width),
                    (1, 4 * hid),
                    (1, width),
                )
            ),
            in_specs=[vmem],
            out_specs=(vmem,) * 5,
            compiler_params=pltpu.CompilerParams(vmem_limit_bytes=8 * MIB),
            name="unpack",
        )(total.reshape(grad_rows, LANES))

    hidden_states = jnp.transpose(outs, (1, 0, 2))[None]
    return (hidden_states, grad_gcn, grad_gbias[0], grad_input, grad_recur, grad_bias[0])


def solution(mesh):
    fine = Mesh(mesh.devices.reshape(4, 2, 8, 4), ("y", "core", "z", "x"))
    return jax.shard_map(
        on_device,
        mesh=fine,
        in_specs=(
            P(SNAP, VTX, None),
            P(SNAP, VTX, None, None, None),
            P(SNAP, VTX, None),
            P(SNAP, VTX),
            P(),
            P(),
            P(),
            P(),
            P(),
            P(VTX, SNAP, None, None),
        ),
        out_specs=(P(VTX, SNAP, None, None), P(), P(), P(), P(), P()),
        check_vma=False,
    )
```

time: 184 us -> 153 us (0.83)
  blocking collectives: 113 us -> 99 us
  Pallas kernels: 28.3 us -> 20.5 us
  starting transfers between devices: 16 us -> 12.2 us
  waiting for transfers between devices: 18.8 us -> 15.9 us
  local copies, waits for them, and re-layouts: 5.95 us -> 3.29 us
    all_to_all x5 -> x4, blocking collectives: 113 us -> 99 us  [the longest x1 50.7 us: on_device(): recv = lax.all_to_all(send, VTX, 0, 0, tiled=True)]
    pallas_call x1 -> x5, Pallas kernels: 14.5 us -> 8.78 us  [the longest x1 6.86 us: on_device(): pl.pallas_call(functools.partial(aggregate, per_peer=blocks), out_shape=j...]
    all_to_all x2, starting transfers between devices: 16 us -> 12.2 us  [the longest x1 8.69 us: on_device(): lax.all_to_all(aggregated.reshape(n_snap, steps_dev, rows, width), SNAP,...]
    all_to_all x2, waiting for transfers between devices: 18.8 us -> 15.9 us  [the longest x1 9.01 us: on_device(): lax.all_to_all(aggregated.reshape(n_snap, steps_dev, rows, width), SNAP,...]
    pallas_call x1, Pallas kernels: 2.96 us -> 1 us  [on_device(): pl.pallas_call(pack_blocks, out_shape=jax.ShapeDtypeStruct((n_vtx, steps_...]
where the time goes in v2:
time: 153 us; the launch traced here: 152 us
  blocking collectives  99 us (65%)
  Pallas kernels  20.5 us (13%)
  waiting for transfers between devices  15.9 us (10%)
  starting transfers between devices  12.2 us (8%)
  local copies, waits for them, and re-layouts  3.29 us (2%)
    all_to_all x1, blocking collectives, on_device(): recv = lax.all_to_all(send, VTX, 0, 0, tiled=True)  50.7 us
    all_to_all x1, blocking collectives, on_device(): want = lax.all_to_all(need, VTX, 0, 0, tiled=True)  20.2 us
    all_to_all x1, blocking collectives, on_device(): part = lax.all_to_all(part, ROUND, 0, 0, tiled=True)  15.3 us
    all_to_all x1, blocking collectives, on_device(): lax.all_to_all(grads.reshape(n_scatter, share, LANES), SCATTER, 0, 0, til...  12.7 us
    pallas_call x1, Pallas kernels, on_device(): pl.pallas_call(recur, out_shape=(jax.ShapeDtypeStruct((steps, rows, hid),...  10.8 us
    all_to_all x1, waiting for transfers between devices, on_device(): lax.all_to_all(aggregated.reshape(n_snap, steps_dev, rows, width), SNAP,...  9.01 us
    all_to_all x1, starting transfers between devices, on_device(): lax.all_to_all(aggregated.reshape(n_snap, steps_dev, rows, width), SNAP,...  8.69 us
    all_to_all x1, waiting for transfers between devices, on_device(): total = lax.all_to_all(part, SCATTER, 0, 0, tiled=True)  6.94 us
  transfers between devices with their start and end apart: 2, of which 2 were waited for; matrix products, arithmetic and copies ran while one was open for 1% of the time, Pallas kernels for 0%

profile of v2, /device:TPU:1, one launch (start us, length us, event | category | flops | bytes accessed | tf_op | source)
XLA Modules:
  0.0 151.8 jit_solution(5033467612728873914)
XLA Ops:
  0.6 0.0 copy-start
  0.6 1.0 copy-done
  1.7 0.0 copy-start.1
  1.7 0.7 copy-done.1
  2.4 0.2 find_requests.1
  2.6 20.2 %all_to_all.36 = s32[32,1,128]{2,1,0:T(1,128)S(1)} all-to-all(s32[32,1,128]{2,1,0:T(1,128)S(1)} %bitcast.29), channel_id=1, replica_groups=mesh['y'=4,'core'=2,'z'=8,'x'=4] {'z','x'}, dimensions={0} | all-to-all | bytes 32768 | tf_op jit(solution)/shard_map/requests/all_to_all | solution.py:258
  22.9 1.0 pack_blocks.1
  23.9 0.0 copy-start.2
  23.9 0.0 copy-start.5
  23.9 50.7 %all_to_all.37.recv_ref = bf16[32,2,128,128]{3,2,1,0:T(8,128)(2,1)S(1)} all-to-all(bf16[32,2,128,128]{3,2,1,0:T(8,128)(2,1)S(1)} %pack_blocks.1), channel_id=1, replica_groups=mesh['y'=4,'core'=2,'z'=8,'x'=4] {'z','x'}, dimensions={0} | all-to-all | bytes 4194304 | tf_op jit(solution)/shard_map/feature_blocks/all_to_all | solution.py:269
  74.6 0.0 copy-done.2
  74.6 0.0 copy-done.5
  74.6 0.0 copy-start.7
  74.6 6.9 %aggregate.1 = bf16[8,2,128,128]{3,2,1,0:T(8,128)(2,1)} custom-call(s32[2,8,16]{2,1,0:T(8,128)S(1)} %copy-done.2, s32[2,8]{1,0:T(2,128)S(1)} %copy-done.5, bf16[32,2,128,128]{3,2,1,0:T(8,128)(2,1)S(1)} %all_to_all.37.recv_ref, bf16[2,8,16,128,128]{4,3,2,1,0:T(8,128)(2,1)} %tile_ref.1), custom_call_target="tpu_custom_call" | custom-call | tf_op jit(solution)/shard_map/aggregate/aggregate/pallas_call | solution.py:272
  81.5 0.0 copy-start.8
  81.5 0.0 copy-start.9
  81.5 0.0 copy-start.3
  81.5 0.0 copy-start.4
  81.6 0.0 copy-start.6
  81.6 8.7 %all-to-all-start.2 = ((bf16[8,2,128,128]{3,2,1,0:T(8,128)(2,1)}), bf16[8,2,128,128]{3,2,1,0:T(8,128)(2,1)S(1)}, u32[]{:S(2)}, u32[]{:S(2)}) async-start(bf16[8,2,128,128]{3,2,1,0:T(8,128)(2,1)} %aggregate.1), calls=%async_computation.2 | async-start | bytes 1048576 | tf_op jit(solution)/shard_map/to_vertices/all_to_all | solution.py:286
  90.3 0.0 copy-done.7
  90.3 0.1 copy.26
  90.4 0.0 copy-done.8
  90.4 0.1 copy.23
  90.5 0.0 copy-done.9
  90.5 0.1 copy.22
  90.7 9.0 %all-to-all-done.2 = bf16[8,2,128,128]{3,2,1,0:T(8,128)(2,1)S(1)} async-done(((bf16[8,2,128,128]{3,2,1,0:T(8,128)(2,1)}), bf16[8,2,128,128]{3,2,1,0:T(8,128)(2,1)S(1)}, u32[]{:S(2)}, u32[]{:S(2)}) %all-to-all-start.2) | async-done | bytes 524320 | tf_op jit(solution)/shard_map/to_vertices/all_to_all | solution.py:286
  99.7 0.0 copy-done.3
  99.7 0.0 copy-done.4
  99.7 0.0 copy-done.6
  99.8 10.8 %recurrence.1 = (bf16[16,128,128]{2,1,0:T(8,128)(2,1)S(1)}, bf16[1280,128]{1,0:T(8,128)(2,1)S(1)}) custom-call(bf16[16,128,128]{2,1,0:T(8,128)(2,1)S(1)} %bitcast.22, bf16[16,128,128]{2,1,0:T(8,128)(2,1)S(1)} %bitcast.23, bf16[128,128]{1,0:T(8,128)(2,1)S(1)} %copy-done.3, f32[1,128]{1,0:T(1,128)S(1)} %bitcast.31, ...), custom_call_target="tpu_custom_call" | custom-call | tf_op jit(solution)/shard_map/recurrence/recurrence/pallas_call | solution.py:291
  110.5 12.7 %all_to_all.38.part_ref = bf16[16,80,128]{2,1,0:T(8,128)(2,1)S(1)} all-to-all(bf16[16,80,128]{2,1,0:T(8,128)(2,1)S(1)} %bitcast.27), channel_id=1, replica_groups=mesh['y'=4,'core'=2,'z'=8,'x'=4] {'y','x'}, dimensions={0} | all-to-all | bytes 655360 | tf_op jit(solution)/shard_map/gradient_sums/all_to_all | solution.py:322
  123.3 0.1 sum_scattered.1
  123.3 15.3 %all_to_all.39.part_ref = bf16[16,80,128]{2,1,0:T(8,128)(2,1)S(1)} all-to-all(bf16[16,80,128]{2,1,0:T(8,128)(2,1)S(1)} %sum_scattered.1), channel_id=1, replica_groups=mesh['y'=4,'core'=2,'z'=8,'x'=4] {'core','z'}, dimensions={0} | all-to-all | bytes 655360 | tf_op jit(solution)/shard_map/gradient_sums/all_to_all | solution.py:333
  138.6 0.8 sum_round.1
  139.4 3.5 %all-to-all-start.5 = ((bf16[16,80,128]{2,1,0:T(8,128)(2,1)}), bf16[16,80,128]{2,1,0:T(8,128)(2,1)S(1)}, u32[]{:S(2)}, u32[]{:S(2)}) async-start(bf16[16,80,128]{2,1,0:T(8,128)(2,1)} %sum_round.1), calls=%async_computation.5 | async-start | bytes 655360 | tf_op jit(solution)/shard_map/gradient_sums/all_to_all | solution.py:342
  142.9 1.1 copy.24
  144.0 6.9 %all-to-all-done.5 = bf16[16,80,128]{2,1,0:T(8,128)(2,1)S(1)} async-done(((bf16[16,80,128]{2,1,0:T(8,128)(2,1)}), bf16[16,80,128]{2,1,0:T(8,128)(2,1)S(1)}, u32[]{:S(2)}, u32[]{:S(2)}) %all-to-all-start.5) | async-done | bytes 327712 | tf_op jit(solution)/shard_map/gradient_sums/all_to_all | solution.py:342
  151.0 0.8 unpack.1
  (2 shorter events, 0.1 us)
Async XLA Ops:
  0.6 1.0 copy-start
  1.7 0.7 copy-start.1
  23.9 50.8 %copy-start.2 = (s32[2,8,16]{2,1,0:T(8,128)S(1)}, s32[2,8,16]{2,1,0:T(8,128)}, u32[]{:S(2)}) copy-start(s32[2,8,16]{2,1,0:T(8,128)} %cols_ref.3) | copy-start | bytes 3076
  23.9 50.7 %copy-start.5 = (s32[2,8]{1,0:T(2,128)S(1)}, s32[2,8]{1,0:T(2,128)}, u32[]{:S(2)}) copy-start(s32[2,8]{1,0:T(2,128)} %count_ref.1) | copy-start | bytes 196
  74.6 15.6 %copy-start.7 = (bf16[1,128,16,128]{3,2,1,0:T(8,128)(2,1)S(1)}, bf16[1,128,16,128]{3,2,1,0:T(8,128)(2,1)}, u32[]{:S(2)}) copy-start(bf16[1,128,16,128]{3,2,1,0:T(8,128)(2,1)} %param.19) | copy-start | bytes 1572868
  81.5 8.9 %copy-start.8 = (bf16[128,512]{1,0:T(8,128)(2,1)S(1)}, bf16[128,512]{1,0:T(8,128)(2,1)}, u32[]{:S(2)}) copy-start(bf16[128,512]{1,0:T(8,128)(2,1)} %param.17) | copy-start | bytes 393220
  81.5 9.0 %copy-start.9 = (bf16[128,512]{1,0:T(8,128)(2,1)S(1)}, bf16[128,512]{1,0:T(8,128)(2,1)}, u32[]{:S(2)}) copy-start(bf16[128,512]{1,0:T(8,128)(2,1)} %param.16) | copy-start | bytes 393220
  81.5 18.2 %copy-start.3 = (bf16[128,128]{1,0:T(8,128)(2,1)S(1)}, bf16[128,128]{1,0:T(8,128)(2,1)}, u32[]{:S(2)}) copy-start(bf16[128,128]{1,0:T(8,128)(2,1)} %gcn_w_ref.1) | copy-start | bytes 98308
  81.5 18.2 %copy-start.4 = (f32[512]{0:T(512)S(1)}, f32[512]{0:T(512)}, u32[]{:S(2)}) copy-start(f32[512]{0:T(512)} %param.18) | copy-start | bytes 6148
  81.6 18.2 %copy-start.6 = (f32[128]{0:T(128)S(1)}, f32[128]{0:T(128)}, u32[]{:S(2)}) copy-start(f32[128]{0:T(128)} %param.15) | copy-start | bytes 1540
  81.6 18.2 %all-to-all-start.2 = ((bf16[8,2,128,128]{3,2,1,0:T(8,128)(2,1)}), bf16[8,2,128,128]{3,2,1,0:T(8,128)(2,1)S(1)}, u32[]{:S(2)}, u32[]{:S(2)}) async-start(bf16[8,2,128,128]{3,2,1,0:T(8,128)(2,1)} %aggregate.1), calls=%async_computation.2 | async-start | bytes 1048576 | tf_op jit(solution)/shard_map/to_vertices/all_to_all | solution.py:286
  139.4 11.6 %all-to-all-start.5 = ((bf16[16,80,128]{2,1,0:T(8,128)(2,1)}), bf16[16,80,128]{2,1,0:T(8,128)(2,1)S(1)}, u32[]{:S(2)}, u32[]{:S(2)}) async-start(bf16[16,80,128]{2,1,0:T(8,128)(2,1)} %sum_round.1), calls=%async_computation.5 | async-start | bytes 655360 | tf_op jit(solution)/shard_map/gradient_sums/all_to_all | solution.py:342

commit v3 on v2

--- a/solution.py
+++ b/solution.py
@@ -20,9 +20,7 @@
     return 0.5 * jnp.tanh(0.5 * value) + 0.5
 
 
-def find_requests(cols_ref, feat_ref, need_ref, held_ref, sem, *, per_peer):
-    copy = pltpu.make_async_copy(feat_ref, held_ref, sem)
-    copy.start()
+def find_requests(cols_ref, need_ref, *, per_peer):
     steps, blocks, slots = cols_ref.shape
     peers = need_ref.shape[0]
     peer_iota = lax.broadcasted_iota(jnp.int32, (peers, slots), 0)
@@ -36,7 +34,27 @@
             found = jnp.maximum(found, jnp.where(inner < per_peer, inner, 0))
         need = jnp.where(lane == step, jnp.max(found, axis=1, keepdims=True), need)
     need_ref[...] = need
+
+
+def stage(from_ref, to_ref, sem):
+    copy = pltpu.make_async_copy(from_ref, to_ref, sem)
+    copy.start()
     copy.wait()
+
+
+def staged(value, limit, name):
+    return pl.pallas_call(
+        stage,
+        out_shape=jax.ShapeDtypeStruct(value.shape, value.dtype),
+        in_specs=[pl.BlockSpec(memory_space=pltpu.HBM)],
+        out_specs=pl.BlockSpec(memory_space=pltpu.VMEM),
+        scratch_shapes=[pltpu.SemaphoreType.DMA],
+        compiler_params=pltpu.CompilerParams(vmem_limit_bytes=limit),
+        cost_estimate=pl.CostEstimate(
+            flops=0, bytes_accessed=2 * value.size * value.dtype.itemsize, transcendentals=0
+        ),
+        name=name,
+    )(value)
 
 
 def pack_blocks(want_ref, feat_ref, send_ref):
@@ -74,7 +92,7 @@
             for slot in range(0, slots, 2):
                 tiles, held = [], []
                 for at in (slot, slot + 1):
-                    peer = jnp.clip(cols_ref[step, block, at] // per_peer, 0, peers - 1)
+                    peer = jnp.clip(lax.div(cols_ref[step, block, at], per_peer), 0, peers - 1)
                     picked = recv_ref[peer, step]
                     tiles.append(held_tiles[step, block, at])
                     held.append(lax.select_n(at < live, jnp.zeros_like(picked), picked))
@@ -118,7 +136,7 @@
         slope_s[t] = squeeze * (1.0 + pre * (1.0 - squeeze))
         return 0
 
-    lax.fori_loop(0, steps, layer, 0)
+    lax.fori_loop(0, steps, layer, 0, unroll=4)
 
     hprev_s[0] = jnp.zeros((rows, hid), BF16)
     cell_s[0] = jnp.zeros((rows, hid), F32)
@@ -143,7 +161,7 @@
         out_ref[t] = out
         return 0
 
-    lax.fori_loop(0, steps, advance, 0)
+    lax.fori_loop(0, steps, advance, 0, unroll=4)
 
     def retreat(k, carried):
         grad_cell, grad_back = carried
@@ -171,7 +189,7 @@
         return grad_cell * gate_keep, back[:, width:]
 
     zero = jnp.zeros((rows, hid), F32)
-    lax.fori_loop(0, steps, retreat, (zero, zero))
+    lax.fori_loop(0, steps, retreat, (zero, zero), unroll=4)
 
     flat_dgates = dgates_s[...].reshape(steps * rows, 4 * hid)
     flat_dpre = dpre_s[...].reshape(steps * rows, width)
@@ -243,18 +261,17 @@
     hbm = pl.BlockSpec(memory_space=pltpu.HBM)
 
     with jax.named_scope("requests"):
-        need, held_features = pl.pallas_call(
+        need = pl.pallas_call(
             functools.partial(find_requests, per_peer=blocks),
-            out_shape=(
-                jax.ShapeDtypeStruct((n_vtx, LANES), jnp.int32),
-                jax.ShapeDtypeStruct((steps_dev, blocks, size, width), BF16),
-            ),
-            in_specs=[vmem, hbm],
-            out_specs=(vmem, vmem),
-            scratch_shapes=[pltpu.SemaphoreType.DMA],
+            out_shape=jax.ShapeDtypeStruct((n_vtx, LANES), jnp.int32),
+            in_specs=[vmem],
+            out_specs=vmem,
             compiler_params=pltpu.CompilerParams(vmem_limit_bytes=8 * MIB),
             name="find_requests",
-        )(tile_cols, features.reshape(steps_dev, blocks, size, width))
+        )(tile_cols)
+        held_features = staged(
+            features.reshape(steps_dev, blocks, size, width), 50 * MIB, "stage_features"
+        )
         want = lax.all_to_all(need, VTX, 0, 0, tiled=True)
 
     with jax.named_scope("feature_blocks"):

time: 153 us -> 150 us (0.980)
  blocking collectives: 99 us -> 78.7 us
  starting transfers between devices: 12.2 us -> 24.1 us
  waiting for transfers between devices: 15.9 us -> 23.4 us
  Pallas kernels: 20.5 us -> 18 us
    all_to_all x1 -> x0, blocking collectives: 20.2 us -> none  [on_device(): want = lax.all_to_all(need, VTX, 0, 0, tiled=True)]
    all_to_all x0 -> x1, starting transfers between devices: none -> 11.9 us  [on_device(): want = lax.all_to_all(need, VTX, 0, 0, tiled=True)]
    all_to_all x0 -> x1, waiting for transfers between devices: none -> 7.41 us  [on_device(): want = lax.all_to_all(need, VTX, 0, 0, tiled=True)]
    pallas_call x1, Pallas kernels: 10.8 us -> 7.94 us  [on_device(): pl.pallas_call(recur, out_shape=(jax.ShapeDtypeStruct((steps, rows, hid),...]
  transfers between devices with their start and end apart: 2 -> 3, of which waited for: 2 -> 3; matrix products, arithmetic and copies ran while one was open for 1% -> 1% of each run, Pallas kernels for 0% -> 0%
where the time goes in v3:
time: 150 us; the launch traced here: 148 us
  blocking collectives  78.7 us (52%)
  starting transfers between devices  24.1 us (16%)
  waiting for transfers between devices  23.4 us (16%)
  Pallas kernels  18 us (12%)
  local copies, waits for them, and re-layouts  3.28 us (2%)
    all_to_all x1, blocking collectives, on_device(): recv = lax.all_to_all(send, VTX, 0, 0, tiled=True)  50.7 us
    all_to_all x1, blocking collectives, on_device(): part = lax.all_to_all(part, ROUND, 0, 0, tiled=True)  15.4 us
    all_to_all x1, blocking collectives, on_device(): lax.all_to_all(grads.reshape(n_scatter, share, LANES), SCATTER, 0, 0, til...  12.6 us
    all_to_all x1, starting transfers between devices, on_device(): want = lax.all_to_all(need, VTX, 0, 0, tiled=True)  11.9 us
    all_to_all x1, waiting for transfers between devices, on_device(): lax.all_to_all(aggregated.reshape(n_snap, steps_dev, rows, width), SNAP,...  9.01 us
    all_to_all x1, starting transfers between devices, on_device(): lax.all_to_all(aggregated.reshape(n_snap, steps_dev, rows, width), SNAP,...  8.7 us
    pallas_call x1, Pallas kernels, on_device(): pl.pallas_call(recur, out_shape=(jax.ShapeDtypeStruct((steps, rows, hid),...  7.94 us
    all_to_all x1, waiting for transfers between devices, on_device(): want = lax.all_to_all(need, VTX, 0, 0, tiled=True)  7.41 us
  transfers between devices with their start and end apart: 3, of which 3 were waited for; matrix products, arithmetic and copies ran while one was open for 1% of the time, Pallas kernels for 0%

profile of v3, /device:TPU:1, one launch (start us, length us, event | category | flops | bytes accessed | tf_op | source)
XLA Modules:
  0.0 148.3 jit_solution(12712079007679176579)
XLA Ops:
  0.6 0.0 copy-start.1
  0.6 0.7 copy-done.1
  1.3 0.8 find_requests.1
  2.1 11.9 %all-to-all-start = ((s32[32,1,128]{2,1,0:T(1,128)}), s32[32,1,128]{2,1,0:T(1,128)S(1)}, u32[]{:S(2)}, u32[]{:S(2)}) async-start(s32[32,1,128]{2,1,0:T(1,128)} %bitcast.1), calls=%async_computation | async-start | bytes 32768 | tf_op jit(solution)/shard_map/requests/all_to_all | solution.py:275
  14.0 0.0 copy-start
  14.0 1.0 copy-done
  15.1 7.4 %all-to-all-done = s32[32,1,128]{2,1,0:T(1,128)S(1)} async-done(((s32[32,1,128]{2,1,0:T(1,128)}), s32[32,1,128]{2,1,0:T(1,128)S(1)}, u32[]{:S(2)}, u32[]{:S(2)}) %all-to-all-start) | async-done | bytes 16416 | tf_op jit(solution)/shard_map/requests/all_to_all | solution.py:275
  22.5 1.0 pack_blocks.1
  23.5 0.0 copy-start.2
  23.5 0.0 copy-start.5
  23.6 50.7 %all_to_all.36.recv_ref = bf16[32,2,128,128]{3,2,1,0:T(8,128)(2,1)S(1)} all-to-all(bf16[32,2,128,128]{3,2,1,0:T(8,128)(2,1)S(1)} %pack_blocks.1), channel_id=1, replica_groups=mesh['y'=4,'core'=2,'z'=8,'x'=4] {'z','x'}, dimensions={0} | all-to-all | bytes 4194304 | tf_op jit(solution)/shard_map/feature_blocks/all_to_all | solution.py:286
  74.3 0.0 copy-done.2
  74.3 0.0 copy-done.5
  74.3 0.0 copy-start.7
  74.3 6.5 %aggregate.1 = bf16[8,2,128,128]{3,2,1,0:T(8,128)(2,1)} custom-call(s32[2,8,16]{2,1,0:T(8,128)S(1)} %copy-done.2, s32[2,8]{1,0:T(2,128)S(1)} %copy-done.5, bf16[32,2,128,128]{3,2,1,0:T(8,128)(2,1)S(1)} %all_to_all.36.recv_ref, bf16[2,8,16,128,128]{4,3,2,1,0:T(8,128)(2,1)} %tile_ref.1), custom_call_target="tpu_custom_call" | custom-call | tf_op jit(solution)/shard_map/aggregate/aggregate/pallas_call | solution.py:289
  80.8 0.0 copy-start.8
  80.8 0.0 copy-start.9
  80.8 0.0 copy-start.3
  80.8 0.0 copy-start.4
  80.9 0.0 copy-start.6
  80.9 8.7 %all-to-all-start.2 = ((bf16[8,2,128,128]{3,2,1,0:T(8,128)(2,1)}), bf16[8,2,128,128]{3,2,1,0:T(8,128)(2,1)S(1)}, u32[]{:S(2)}, u32[]{:S(2)}) async-start(bf16[8,2,128,128]{3,2,1,0:T(8,128)(2,1)} %aggregate.1), calls=%async_computation.2 | async-start | bytes 1048576 | tf_op jit(solution)/shard_map/to_vertices/all_to_all | solution.py:303
  89.6 0.0 copy-done.7
  89.6 0.1 copy.26
  89.7 0.0 copy-done.8
  89.7 0.1 copy.23
  89.8 0.0 copy-done.9
  89.8 0.1 copy.22
  90.0 9.0 %all-to-all-done.2 = bf16[8,2,128,128]{3,2,1,0:T(8,128)(2,1)S(1)} async-done(((bf16[8,2,128,128]{3,2,1,0:T(8,128)(2,1)}), bf16[8,2,128,128]{3,2,1,0:T(8,128)(2,1)S(1)}, u32[]{:S(2)}, u32[]{:S(2)}) %all-to-all-start.2) | async-done | bytes 524320 | tf_op jit(solution)/shard_map/to_vertices/all_to_all | solution.py:303
  99.0 0.0 copy-done.3
  99.0 0.0 copy-done.4
  99.1 0.0 copy-done.6
  99.1 7.9 %recurrence.1 = (bf16[16,128,128]{2,1,0:T(8,128)(2,1)S(1)}, bf16[1280,128]{1,0:T(8,128)(2,1)S(1)}) custom-call(bf16[16,128,128]{2,1,0:T(8,128)(2,1)S(1)} %bitcast.22, bf16[16,128,128]{2,1,0:T(8,128)(2,1)S(1)} %bitcast.23, bf16[128,128]{1,0:T(8,128)(2,1)S(1)} %copy-done.3, f32[1,128]{1,0:T(1,128)S(1)} %bitcast.30, ...), custom_call_target="tpu_custom_call" | custom-call | tf_op jit(solution)/shard_map/recurrence/recurrence/pallas_call | solution.py:308
  107.0 12.6 %all_to_all.37.part_ref = bf16[16,80,128]{2,1,0:T(8,128)(2,1)S(1)} all-to-all(bf16[16,80,128]{2,1,0:T(8,128)(2,1)S(1)} %bitcast.27), channel_id=1, replica_groups=mesh['y'=4,'core'=2,'z'=8,'x'=4] {'y','x'}, dimensions={0} | all-to-all | bytes 655360 | tf_op jit(solution)/shard_map/gradient_sums/all_to_all | solution.py:339
  119.6 0.1 sum_scattered.1
  119.6 15.4 %all_to_all.38.part_ref = bf16[16,80,128]{2,1,0:T(8,128)(2,1)S(1)} all-to-all(bf16[16,80,128]{2,1,0:T(8,128)(2,1)S(1)} %sum_scattered.1), channel_id=1, replica_groups=mesh['y'=4,'core'=2,'z'=8,'x'=4] {'core','z'}, dimensions={0} | all-to-all | bytes 655360 | tf_op jit(solution)/shard_map/gradient_sums/all_to_all | solution.py:350
  135.0 0.8 sum_round.1
  135.8 3.5 %all-to-all-start.5 = ((bf16[16,80,128]{2,1,0:T(8,128)(2,1)}), bf16[16,80,128]{2,1,0:T(8,128)(2,1)S(1)}, u32[]{:S(2)}, u32[]{:S(2)}) async-start(bf16[16,80,128]{2,1,0:T(8,128)(2,1)} %sum_round.1), calls=%async_computation.5 | async-start | bytes 655360 | tf_op jit(solution)/shard_map/gradient_sums/all_to_all | solution.py:359
  139.4 1.1 copy.24
  140.5 6.9 %all-to-all-done.5 = bf16[16,80,128]{2,1,0:T(8,128)(2,1)S(1)} async-done(((bf16[16,80,128]{2,1,0:T(8,128)(2,1)}), bf16[16,80,128]{2,1,0:T(8,128)(2,1)S(1)}, u32[]{:S(2)}, u32[]{:S(2)}) %all-to-all-start.5) | async-done | bytes 327712 | tf_op jit(solution)/shard_map/gradient_sums/all_to_all | solution.py:359
  147.4 0.8 unpack.1
  (3 shorter events, 0.1 us)
Async XLA Ops:
  0.6 0.7 copy-start.1
  2.1 20.4 %all-to-all-start = ((s32[32,1,128]{2,1,0:T(1,128)}), s32[32,1,128]{2,1,0:T(1,128)S(1)}, u32[]{:S(2)}, u32[]{:S(2)}) async-start(s32[32,1,128]{2,1,0:T(1,128)} %bitcast.1), calls=%async_computation | async-start | bytes 32768 | tf_op jit(solution)/shard_map/requests/all_to_all | solution.py:275
  14.0 1.0 copy-start
  23.5 50.8 %copy-start.2 = (s32[2,8,16]{2,1,0:T(8,128)S(1)}, s32[2,8,16]{2,1,0:T(8,128)}, u32[]{:S(2)}) copy-start(s32[2,8,16]{2,1,0:T(8,128)} %cols_ref.3) | copy-start | bytes 3076
  23.5 50.7 %copy-start.5 = (s32[2,8]{1,0:T(2,128)S(1)}, s32[2,8]{1,0:T(2,128)}, u32[]{:S(2)}) copy-start(s32[2,8]{1,0:T(2,128)} %count_ref.1) | copy-start | bytes 196
  74.3 15.3 %copy-start.7 = (bf16[1,128,16,128]{3,2,1,0:T(8,128)(2,1)S(1)}, bf16[1,128,16,128]{3,2,1,0:T(8,128)(2,1)}, u32[]{:S(2)}) copy-start(bf16[1,128,16,128]{3,2,1,0:T(8,128)(2,1)} %param.19) | copy-start | bytes 1572868
  80.8 8.9 %copy-start.8 = (bf16[128,512]{1,0:T(8,128)(2,1)S(1)}, bf16[128,512]{1,0:T(8,128)(2,1)}, u32[]{:S(2)}) copy-start(bf16[128,512]{1,0:T(8,128)(2,1)} %param.17) | copy-start | bytes 393220
  80.8 9.0 %copy-start.9 = (bf16[128,512]{1,0:T(8,128)(2,1)S(1)}, bf16[128,512]{1,0:T(8,128)(2,1)}, u32[]{:S(2)}) copy-start(bf16[128,512]{1,0:T(8,128)(2,1)} %param.16) | copy-start | bytes 393220
  80.8 18.2 %copy-start.3 = (bf16[128,128]{1,0:T(8,128)(2,1)S(1)}, bf16[128,128]{1,0:T(8,128)(2,1)}, u32[]{:S(2)}) copy-start(bf16[128,128]{1,0:T(8,128)(2,1)} %gcn_w_ref.1) | copy-start | bytes 98308
  80.8 18.2 %copy-start.4 = (f32[512]{0:T(512)S(1)}, f32[512]{0:T(512)}, u32[]{:S(2)}) copy-start(f32[512]{0:T(512)} %param.18) | copy-start | bytes 6148
  80.9 18.2 %copy-start.6 = (f32[128]{0:T(128)S(1)}, f32[128]{0:T(128)}, u32[]{:S(2)}) copy-start(f32[128]{0:T(128)} %param.15) | copy-start | bytes 1540
  80.9 18.2 %all-to-all-start.2 = ((bf16[8,2,128,128]{3,2,1,0:T(8,128)(2,1)}), bf16[8,2,128,128]{3,2,1,0:T(8,128)(2,1)S(1)}, u32[]{:S(2)}, u32[]{:S(2)}) async-start(bf16[8,2,128,128]{3,2,1,0:T(8,128)(2,1)} %aggregate.1), calls=%async_computation.2 | async-start | bytes 1048576 | tf_op jit(solution)/shard_map/to_vertices/all_to_all | solution.py:303
  135.8 11.6 %all-to-all-start.5 = ((bf16[16,80,128]{2,1,0:T(8,128)(2,1)}), bf16[16,80,128]{2,1,0:T(8,128)(2,1)S(1)}, u32[]{:S(2)}, u32[]{:S(2)}) async-start(bf16[16,80,128]{2,1,0:T(8,128)(2,1)} %sum_round.1), calls=%async_computation.5 | async-start | bytes 655360 | tf_op jit(solution)/shard_map/gradient_sums/all_to_all | solution.py:359

commit v4 on v3

--- a/solution.py
+++ b/solution.py
@@ -13,7 +13,7 @@
 MIB = 1024 * 1024
 LANES = 128
 VTX, SNAP = ("z", "x"), ("y", "core")
-SCATTER, ROUND = ("y", "x"), ("core", "z")
+SCATTER, ROUND, PAIR = ("x", "y"), "z", "core"
 
 
 def sigmoid(value):
@@ -108,6 +108,7 @@
 
 
 def recur(
+    core_ref,
     agg_ref,
     hgrad_ref,
     gcn_w_ref,
@@ -116,7 +117,8 @@
     bias_ref,
     w_back_ref,
     out_ref,
-    grads_ref,
+    keep_ref,
+    send_ref,
     layer_s,
     slope_s,
     gates_s,
@@ -125,6 +127,7 @@
     hprev_s,
     dgates_s,
     dpre_s,
+    grads_s,
 ):
     steps, rows, width = agg_ref.shape
     hid = width
@@ -202,9 +205,7 @@
     def put(at, value):
         height = value.shape[0]
         for k in range(value.shape[1] // LANES):
-            grads_ref[pl.ds(at + k * height, height), :] = value[
-                :, k * LANES : (k + 1) * LANES
-            ].astype(BF16)
+            grads_s[pl.ds(at + k * height, height), :] = value[:, k * LANES : (k + 1) * LANES]
         return at + value.shape[1] // LANES * height
 
     ones = jnp.ones((8, steps * rows), BF16)
@@ -213,9 +214,15 @@
     at = put(at, over_rows(agg_ref[...].reshape(steps * rows, width), flat_dpre))
     at = put(at, jnp.dot(ones, flat_dgates, preferred_element_type=F32))
     at = put(at, jnp.dot(ones, flat_dpre, preferred_element_type=F32))
-    grads_ref[pl.ds(at, grads_ref.shape[0] - at), :] = jnp.zeros(
-        (grads_ref.shape[0] - at, LANES), BF16
-    )
+    grads_s[pl.ds(at, grads_s.shape[0] - at), :] = jnp.zeros((grads_s.shape[0] - at, LANES), F32)
+    half = keep_ref.shape[0]
+    core = core_ref[0]
+    keep_ref[...] = grads_s[pl.ds(pl.multiple_of(core * half, 8), half), :]
+    send_ref[...] = grads_s[pl.ds(pl.multiple_of((1 - core) * half, 8), half), :]
+
+
+def sum_pair(left_ref, right_ref, out_ref):
+    out_ref[...] = (left_ref[...] + right_ref[...]).astype(out_ref.dtype)
 
 
 def sum_parts(part_ref, out_ref):
@@ -223,15 +230,18 @@
     out_ref[...] = jnp.broadcast_to(total.astype(out_ref.dtype)[None], out_ref.shape)
 
 
-def unpack(total_ref, *out_refs):
+def unpack(core_ref, mine_ref, other_ref, *refs):
+    out_refs, total_ref = refs[:-1], refs[-1]
+    half = mine_ref.shape[0]
+    core = core_ref[0]
+    total_ref[pl.ds(pl.multiple_of(core * half, 8), half), :] = mine_ref[...].astype(F32)
+    total_ref[pl.ds(pl.multiple_of((1 - core) * half, 8), half), :] = other_ref[...].astype(F32)
     at = 0
     for out_ref in out_refs:
         height, columns = out_ref.shape
         taken = max(height, 8)
         for k in range(columns // LANES):
-            out_ref[:, k * LANES : (k + 1) * LANES] = total_ref[pl.ds(at, taken), :].astype(F32)[
-                :height
-            ]
+            out_ref[:, k * LANES : (k + 1) * LANES] = total_ref[pl.ds(at, taken), :][:height]
             at += taken
 
 
@@ -254,8 +264,9 @@
     steps, rows = steps_dev * n_snap, local_verts // n_snap
     n_scatter, n_round = lax.axis_size(SCATTER), lax.axis_size(ROUND)
     held_rows = (2 * 4 * hid + width) * width // LANES + 8 * (4 * hid + width) // LANES
-    share = -(-held_rows // (8 * n_scatter)) * 8
-    grad_rows = n_scatter * share
+    share = -(-held_rows // (2 * 8 * n_scatter)) * 8
+    half_rows = n_scatter * share
+    core = lax.axis_index(PAIR).astype(jnp.int32).reshape(1)
     smem = pl.BlockSpec(memory_space=pltpu.SMEM)
     vmem = pl.BlockSpec(memory_space=pltpu.VMEM)
     hbm = pl.BlockSpec(memory_space=pltpu.HBM)
@@ -305,14 +316,15 @@
         ).reshape(steps, rows, width)
 
     with jax.named_scope("recurrence"):
-        outs, grads = pl.pallas_call(
+        outs, keep, away = pl.pallas_call(
             recur,
             out_shape=(
                 jax.ShapeDtypeStruct((steps, rows, hid), BF16),
-                jax.ShapeDtypeStruct((grad_rows, LANES), BF16),
+                jax.ShapeDtypeStruct((half_rows, LANES), F32),
+                jax.ShapeDtypeStruct((half_rows, LANES), F32),
             ),
-            in_specs=[vmem] * 7,
-            out_specs=(vmem, vmem),
+            in_specs=[smem] + [vmem] * 7,
+            out_specs=(vmem, vmem, vmem),
             scratch_shapes=[
                 pltpu.VMEM((steps, rows, width), BF16),
                 pltpu.VMEM((steps, rows, width), F32),
@@ -322,10 +334,12 @@
                 pltpu.VMEM((steps + 1, rows, hid), BF16),
                 pltpu.VMEM((steps, rows, 4 * hid), BF16),
                 pltpu.VMEM((steps, rows, width), BF16),
+                pltpu.VMEM((2 * half_rows, LANES), F32),
             ],
             compiler_params=pltpu.CompilerParams(vmem_limit_bytes=40 * MIB),
             name="recurrence",
         )(
+            core,
             by_step,
             jnp.transpose(hidden_grad[0], (1, 0, 2)),
             gcn_weight,
@@ -336,8 +350,16 @@
         )
 
     with jax.named_scope("gradient_sums"):
+        part = pl.pallas_call(
+            sum_pair,
+            out_shape=jax.ShapeDtypeStruct((half_rows, LANES), BF16),
+            in_specs=[vmem, vmem],
+            out_specs=vmem,
+            compiler_params=pltpu.CompilerParams(vmem_limit_bytes=8 * MIB),
+            name="sum_pair",
+        )(keep, lax.ppermute(away, PAIR, ((0, 1), (1, 0))))
         part = lax.all_to_all(
-            grads.reshape(n_scatter, share, LANES), SCATTER, 0, 0, tiled=True
+            part.reshape(n_scatter, share, LANES), SCATTER, 0, 0, tiled=True
         )
         part = pl.pallas_call(
             sum_parts,
@@ -356,7 +378,8 @@
             compiler_params=pltpu.CompilerParams(vmem_limit_bytes=8 * MIB),
             name="sum_round",
         )(part)
-        total = lax.all_to_all(part, SCATTER, 0, 0, tiled=True)
+        mine = lax.all_to_all(part, SCATTER, 0, 0, tiled=True).reshape(half_rows, LANES)
+        other = lax.ppermute(mine, PAIR, ((0, 1), (1, 0)))
         grad_input, grad_recur, grad_gcn, grad_bias, grad_gbias = pl.pallas_call(
             unpack,
             out_shape=tuple(
@@ -369,11 +392,12 @@
                     (1, width),
                 )
             ),
-            in_specs=[vmem],
+            in_specs=[smem, vmem, vmem],
             out_specs=(vmem,) * 5,
+            scratch_shapes=[pltpu.VMEM((2 * half_rows, LANES), F32)],
             compiler_params=pltpu.CompilerParams(vmem_limit_bytes=8 * MIB),
             name="unpack",
-        )(total.reshape(grad_rows, LANES))
+        )(core, mine, other)
 
     hidden_states = jnp.transpose(outs, (1, 0, 2))[None]
     return (hidden_states, grad_gcn, grad_gbias[0], grad_input, grad_recur, grad_bias[0])

time: 150 us -> 147 us (0.980); the launches traced: 148 us -> 147 us
  waiting for transfers between devices: 23.4 us -> 17.7 us
  blocking collectives: 78.7 us -> 82 us
  starting transfers between devices: 24.1 us -> 25.6 us
    all_to_all x1 -> x2, blocking collectives: 12.6 us -> 21.4 us  [the longest x1 11.3 us: on_device(): lax.all_to_all(part.reshape(n_scatter, share, LANES), SCATTER, 0, 0, tile...]
    all_to_all x1 -> x0, waiting for transfers between devices: 6.94 us -> none  [on_device(): total = lax.all_to_all(part, SCATTER, 0, 0, tiled=True)]
    all_to_all x1, blocking collectives: 15.4 us -> 9.88 us  [on_device(): part = lax.all_to_all(part, ROUND, 0, 0, tiled=True)]
    ppermute x0 -> x2, starting transfers between devices: none -> 5.06 us  [the longest x1 4.09 us: on_device(): other = lax.ppermute(mine, PAIR, ((0, 1), (1, 0)))]
    all_to_all x1 -> x0, starting transfers between devices: 3.54 us -> none  [on_device(): total = lax.all_to_all(part, SCATTER, 0, 0, tiled=True)]
  transfers between devices with their start and end apart: 3 -> 4, of which waited for: 3 -> 3; matrix products, arithmetic and copies ran while one was open for 1% -> 1% of each run, Pallas kernels for 0% -> 0%
where the time goes in v4:
time: 147 us
  blocking collectives  82 us (56%)
  starting transfers between devices  25.6 us (17%)
  waiting for transfers between devices  17.7 us (12%)
  Pallas kernels  17.3 us (12%)
  local copies, waits for them, and re-layouts  3.28 us (2%)
    all_to_all x1, blocking collectives, on_device(): recv = lax.all_to_all(send, VTX, 0, 0, tiled=True)  50.7 us
    all_to_all x1, starting transfers between devices, on_device(): want = lax.all_to_all(need, VTX, 0, 0, tiled=True)  11.9 us
    all_to_all x1, blocking collectives, on_device(): lax.all_to_all(part.reshape(n_scatter, share, LANES), SCATTER, 0, 0, tile...  11.3 us
    all_to_all x1, blocking collectives, on_device(): lax.all_to_all(part, SCATTER, 0, 0, tiled=True).reshape(half_rows, LANES)  10.1 us
    all_to_all x1, blocking collectives, on_device(): part = lax.all_to_all(part, ROUND, 0, 0, tiled=True)  9.88 us
    all_to_all x1, waiting for transfers between devices, on_device(): lax.all_to_all(aggregated.reshape(n_snap, steps_dev, rows, width), SNAP,...  9.01 us
    all_to_all x1, starting transfers between devices, on_device(): lax.all_to_all(aggregated.reshape(n_snap, steps_dev, rows, width), SNAP,...  8.7 us
    pallas_call x1, Pallas kernels, on_device(): pl.pallas_call(recur, out_shape=(jax.ShapeDtypeStruct((steps, rows, hid),...  7.97 us
  transfers between devices with their start and end apart: 4, of which 3 were waited for; matrix products, arithmetic and copies ran while one was open for 1% of the time, Pallas kernels for 0%

profile of v4, /device:TPU:1, one launch (start us, length us, event | category | flops | bytes accessed | tf_op | source)
XLA Modules:
  0.0 146.8 jit_solution(16030068496025356886)
XLA Ops:
  0.6 0.0 copy-start.1
  0.6 0.7 copy-done.1
  1.3 0.8 find_requests.1
  2.1 11.9 %all-to-all-start = ((s32[32,1,128]{2,1,0:T(1,128)}), s32[32,1,128]{2,1,0:T(1,128)S(1)}, u32[]{:S(2)}, u32[]{:S(2)}) async-start(s32[32,1,128]{2,1,0:T(1,128)} %bitcast.2), calls=%async_computation | async-start | bytes 32768 | tf_op jit(solution)/shard_map/requests/all_to_all | solution.py:286
  14.0 0.0 copy-start
  14.0 1.0 copy-done
  15.1 7.4 %all-to-all-done = s32[32,1,128]{2,1,0:T(1,128)S(1)} async-done(((s32[32,1,128]{2,1,0:T(1,128)}), s32[32,1,128]{2,1,0:T(1,128)S(1)}, u32[]{:S(2)}, u32[]{:S(2)}) %all-to-all-start) | async-done | bytes 16416 | tf_op jit(solution)/shard_map/requests/all_to_all | solution.py:286
  22.5 1.0 pack_blocks.1
  23.5 0.0 copy-start.2
  23.5 0.0 copy-start.5
  23.6 50.7 %all_to_all.36.recv_ref = bf16[32,2,128,128]{3,2,1,0:T(8,128)(2,1)S(1)} all-to-all(bf16[32,2,128,128]{3,2,1,0:T(8,128)(2,1)S(1)} %pack_blocks.1), channel_id=1, replica_groups=mesh['y'=4,'core'=2,'z'=8,'x'=4] {'z','x'}, dimensions={0} | all-to-all | bytes 4194304 | tf_op jit(solution)/shard_map/feature_blocks/all_to_all | solution.py:297
  74.3 0.0 copy-done.2
  74.3 0.0 copy-done.5
  74.3 0.0 copy-start.7
  74.3 6.5 %aggregate.1 = bf16[8,2,128,128]{3,2,1,0:T(8,128)(2,1)} custom-call(s32[2,8,16]{2,1,0:T(8,128)S(1)} %copy-done.2, s32[2,8]{1,0:T(2,128)S(1)} %copy-done.5, bf16[32,2,128,128]{3,2,1,0:T(8,128)(2,1)S(1)} %all_to_all.36.recv_ref, bf16[2,8,16,128,128]{4,3,2,1,0:T(8,128)(2,1)} %tile_ref.1), custom_call_target="tpu_custom_call" | custom-call | tf_op jit(solution)/shard_map/aggregate/aggregate/pallas_call | solution.py:300
  80.8 0.0 copy-start.9
  80.8 0.0 copy-start.8
  80.8 0.0 copy-start.3
  80.8 0.0 copy-start.4
  80.9 0.0 copy-start.6
  80.9 8.7 %all-to-all-start.2 = ((bf16[8,2,128,128]{3,2,1,0:T(8,128)(2,1)}), bf16[8,2,128,128]{3,2,1,0:T(8,128)(2,1)S(1)}, u32[]{:S(2)}, u32[]{:S(2)}) async-start(bf16[8,2,128,128]{3,2,1,0:T(8,128)(2,1)} %aggregate.1), calls=%async_computation.2 | async-start | bytes 1048576 | tf_op jit(solution)/shard_map/to_vertices/all_to_all | solution.py:314
  89.6 0.0 copy-done.7
  89.6 0.1 copy.26
  89.7 0.0 copy-done.9
  89.7 0.1 copy.22
  89.8 0.0 copy-done.8
  89.8 0.1 copy.23
  90.0 9.0 %all-to-all-done.2 = bf16[8,2,128,128]{3,2,1,0:T(8,128)(2,1)S(1)} async-done(((bf16[8,2,128,128]{3,2,1,0:T(8,128)(2,1)}), bf16[8,2,128,128]{3,2,1,0:T(8,128)(2,1)S(1)}, u32[]{:S(2)}, u32[]{:S(2)}) %all-to-all-start.2) | async-done | bytes 524320 | tf_op jit(solution)/shard_map/to_vertices/all_to_all | solution.py:314
  99.0 0.0 copy-done.3
  99.0 0.0 copy-done.4
  99.1 0.0 copy-done.6
  99.1 8.0 %recurrence.1 = (bf16[16,128,128]{2,1,0:T(8,128)(2,1)S(1)}, f32[640,128]{1,0:T(8,128)S(1)}, f32[640,128]{1,0:T(8,128)S(1)}) custom-call(s32[1]{0:T(128)} %bitcast.core_ref, bf16[16,128,128]{2,1,0:T(8,128)(2,1)S(1)} %bitcast.23, bf16[16,128,128]{2,1,0:T(8,128)(2,1)S(1)} %bitcast.24, bf16[128,128]{1,0:T(8,128)(2,1)S(1)} %copy-done.3, f32[1,128]{1,0:T(1,128)S(1)} %bitcast.32, ...), custom_call_target="tpu_custom_call" | custom-call | tf_op jit(solution)/shard_map/recurrence/recurrence/pallas_call | solution.py:319
  107.0 1.0 collective-permute-start
  108.0 1.3 collective-permute-done.right_ref
  109.3 0.1 sum_pair.1
  109.3 11.3 %all_to_all.37.part_ref = bf16[16,40,128]{2,1,0:T(8,128)(2,1)S(1)} all-to-all(bf16[16,40,128]{2,1,0:T(8,128)(2,1)S(1)} %bitcast.27), channel_id=1, replica_groups=mesh['y'=4,'core'=2,'z'=8,'x'=4] {'x','y'}, dimensions={0} | all-to-all | bytes 327680 | tf_op jit(solution)/shard_map/gradient_sums/all_to_all | solution.py:361
  120.7 9.9 %all_to_all.38.part_ref = bf16[8,40,128]{2,1,0:T(8,128)(2,1)S(1)} all-to-all(bf16[8,40,128]{2,1,0:T(8,128)(2,1)S(1)} %sum_scattered.1), channel_id=1, replica_groups=mesh['y'=4,'core'=2,'z'=8,'x'=4] {'z'}, dimensions={0} | all-to-all | bytes 163840 | tf_op jit(solution)/shard_map/gradient_sums/all_to_all | solution.py:372
  130.6 10.1 %all_to_all.39 = bf16[16,40,128]{2,1,0:T(8,128)(2,1)S(1)} all-to-all(bf16[16,40,128]{2,1,0:T(8,128)(2,1)S(1)} %sum_round.1), channel_id=1, replica_groups=mesh['y'=4,'core'=2,'z'=8,'x'=4] {'x','y'}, dimensions={0} | all-to-all | bytes 327680 | tf_op jit(solution)/shard_map/gradient_sums/all_to_all | solution.py:381
  140.7 4.1 %collective-permute-start.1 = (bf16[640,128]{1,0:T(8,128)(2,1)S(1)}, bf16[640,128]{1,0:T(8,128)(2,1)S(1)}, u32[]{:S(2)}, u32[]{:S(2)}) collective-permute-start(bf16[640,128]{1,0:T(8,128)(2,1)S(1)} %bitcast.25), channel_id=1, source_target_pairs={{0,32},{32,0},{1,33},{33,1},{2,34},{34,2},{3,35},{35,3},{4,36},{36... | collective-permute-start | bytes 491528 | tf_op jit(solution)/shard_map/gradient_sums/ppermute | solution.py:382
  144.8 1.1 copy.24
  145.9 0.0 collective-permute-done.1.other_ref
  145.9 0.9 unpack.1
  (5 shorter events, 0.1 us)
Async XLA Ops:
  0.6 0.7 copy-start.1
  2.1 20.4 %all-to-all-start = ((s32[32,1,128]{2,1,0:T(1,128)}), s32[32,1,128]{2,1,0:T(1,128)S(1)}, u32[]{:S(2)}, u32[]{:S(2)}) async-start(s32[32,1,128]{2,1,0:T(1,128)} %bitcast.2), calls=%async_computation | async-start | bytes 32768 | tf_op jit(solution)/shard_map/requests/all_to_all | solution.py:286
  14.0 1.0 copy-start
  23.5 50.8 %copy-start.2 = (s32[2,8,16]{2,1,0:T(8,128)S(1)}, s32[2,8,16]{2,1,0:T(8,128)}, u32[]{:S(2)}) copy-start(s32[2,8,16]{2,1,0:T(8,128)} %cols_ref.3) | copy-start | bytes 3076
  23.5 50.7 %copy-start.5 = (s32[2,8]{1,0:T(2,128)S(1)}, s32[2,8]{1,0:T(2,128)}, u32[]{:S(2)}) copy-start(s32[2,8]{1,0:T(2,128)} %count_ref.1) | copy-start | bytes 196
  74.3 15.3 %copy-start.7 = (bf16[1,128,16,128]{3,2,1,0:T(8,128)(2,1)S(1)}, bf16[1,128,16,128]{3,2,1,0:T(8,128)(2,1)}, u32[]{:S(2)}) copy-start(bf16[1,128,16,128]{3,2,1,0:T(8,128)(2,1)} %param.19) | copy-start | bytes 1572868
  80.8 8.9 %copy-start.9 = (bf16[128,512]{1,0:T(8,128)(2,1)S(1)}, bf16[128,512]{1,0:T(8,128)(2,1)}, u32[]{:S(2)}) copy-start(bf16[128,512]{1,0:T(8,128)(2,1)} %param.16) | copy-start | bytes 393220
  80.8 9.0 %copy-start.8 = (bf16[128,512]{1,0:T(8,128)(2,1)S(1)}, bf16[128,512]{1,0:T(8,128)(2,1)}, u32[]{:S(2)}) copy-start(bf16[128,512]{1,0:T(8,128)(2,1)} %param.17) | copy-start | bytes 393220
  80.8 18.2 %copy-start.3 = (bf16[128,128]{1,0:T(8,128)(2,1)S(1)}, bf16[128,128]{1,0:T(8,128)(2,1)}, u32[]{:S(2)}) copy-start(bf16[128,128]{1,0:T(8,128)(2,1)} %gcn_w_ref.1) | copy-start | bytes 98308
  80.8 18.2 %copy-start.4 = (f32[512]{0:T(512)S(1)}, f32[512]{0:T(512)}, u32[]{:S(2)}) copy-start(f32[512]{0:T(512)} %param.18) | copy-start | bytes 6148
  80.9 18.2 %copy-start.6 = (f32[128]{0:T(128)S(1)}, f32[128]{0:T(128)}, u32[]{:S(2)}) copy-start(f32[128]{0:T(128)} %param.15) | copy-start | bytes 1540
  80.9 18.2 %all-to-all-start.2 = ((bf16[8,2,128,128]{3,2,1,0:T(8,128)(2,1)}), bf16[8,2,128,128]{3,2,1,0:T(8,128)(2,1)S(1)}, u32[]{:S(2)}, u32[]{:S(2)}) async-start(bf16[8,2,128,128]{3,2,1,0:T(8,128)(2,1)} %aggregate.1), calls=%async_computation.2 | async-start | bytes 1048576 | tf_op jit(solution)/shard_map/to_vertices/all_to_all | solution.py:314
  107.0 2.2 %collective-permute-start = (f32[640,128]{1,0:T(8,128)S(1)}, f32[640,128]{1,0:T(8,128)S(1)}, u32[]{:S(2)}, u32[]{:S(2)}) collective-permute-start(f32[640,128]{1,0:T(8,128)S(1)} %get-tuple-element.16), channel_id=1, source_target_pairs={{0,32},{32,0},{1,33},{33,1},{2,34},{34,2},{3,35},{35,3},{4,36},{36... | collective-permute-start | bytes 983048 | tf_op jit(solution)/shard_map/gradient_sums/ppermute | solution.py:360
  140.7 5.2 %collective-permute-start.1 = (bf16[640,128]{1,0:T(8,128)(2,1)S(1)}, bf16[640,128]{1,0:T(8,128)(2,1)S(1)}, u32[]{:S(2)}, u32[]{:S(2)}) collective-permute-start(bf16[640,128]{1,0:T(8,128)(2,1)S(1)} %bitcast.25), channel_id=1, source_target_pairs={{0,32},{32,0},{1,33},{33,1},{2,34},{34,2},{3,35},{35,3},{4,36},{36... | collective-permute-start | bytes 491528 | tf_op jit(solution)/shard_map/gradient_sums/ppermute | solution.py:382

commit v5 on v4

--- a/solution.py
+++ b/solution.py
@@ -57,7 +57,8 @@
     )(value)
 
 
-def pack_blocks(want_ref, feat_ref, send_ref):
+def pack_blocks(want_ref, feat_ref, tile_ref, send_ref):
+    del tile_ref
     peers, steps = send_ref.shape[:2]
     per_peer = feat_ref.shape[1]
 
@@ -70,22 +71,11 @@
     lax.fori_loop(0, peers, fill, 0, unroll=4)
 
 
-def aggregate(cols_ref, count_ref, recv_ref, tile_ref, out_ref, held_tiles, sems, *, per_peer):
+def aggregate(cols_ref, count_ref, recv_ref, tile_ref, out_ref, *, per_peer):
     steps, blocks, slots, size = tile_ref.shape[:4]
     peers, width = recv_ref.shape[0], recv_ref.shape[3]
 
-    def fetch(step, block):
-        return pltpu.make_async_copy(
-            tile_ref.at[step, block], held_tiles.at[step, block], sems.at[step, block]
-        )
-
-    for block in range(blocks):
-        for step in range(steps):
-            fetch(step, block).start()
-
     def one_block(block, _):
-        for step in range(steps):
-            fetch(step, block).wait()
         for step in range(steps):
             live = count_ref[step, block]
             total = jnp.zeros((size, width), F32)
@@ -94,7 +84,7 @@
                 for at in (slot, slot + 1):
                     peer = jnp.clip(lax.div(cols_ref[step, block, at], per_peer), 0, peers - 1)
                     picked = recv_ref[peer, step]
-                    tiles.append(held_tiles[step, block, at])
+                    tiles.append(tile_ref[step, block, at])
                     held.append(lax.select_n(at < live, jnp.zeros_like(picked), picked))
                 total = total + jnp.dot(
                     jnp.concatenate(tiles, axis=1),
@@ -289,24 +279,20 @@
         send = pl.pallas_call(
             pack_blocks,
             out_shape=jax.ShapeDtypeStruct((n_vtx, steps_dev, size, width), BF16),
-            in_specs=[smem, vmem],
-            out_specs=vmem,
-            compiler_params=pltpu.CompilerParams(vmem_limit_bytes=8 * MIB),
+            in_specs=[smem, vmem, hbm],
+            out_specs=vmem,
+            compiler_params=pltpu.CompilerParams(vmem_limit_bytes=46 * MIB),
             name="pack_blocks",
-        )(want, held_features)
+        )(want, held_features, tile_vals)
         recv = lax.all_to_all(send, VTX, 0, 0, tiled=True)
 
     with jax.named_scope("aggregate"):
         aggregated = pl.pallas_call(
             functools.partial(aggregate, per_peer=blocks),
             out_shape=jax.ShapeDtypeStruct((blocks, steps_dev, size, width), BF16),
-            in_specs=[smem, smem, vmem, hbm],
-            out_specs=vmem,
-            scratch_shapes=[
-                pltpu.VMEM(tile_vals.shape, BF16),
-                pltpu.SemaphoreType.DMA((steps_dev, blocks)),
-            ],
-            compiler_params=pltpu.CompilerParams(vmem_limit_bytes=50 * MIB),
+            in_specs=[smem, smem, vmem, vmem],
+            out_specs=vmem,
+            compiler_params=pltpu.CompilerParams(vmem_limit_bytes=8 * MIB),
             name="aggregate",
         )(tile_cols, tile_count, recv, tile_vals)
 

time: 147 us -> 146 us (level)
    unnamed x24 -> x26, local copies, waits for them, and re-layouts: 3.28 us -> 3.28 us
where the time goes in v5:
time: 146 us
  blocking collectives  82.3 us (56%)
  starting transfers between devices  25.6 us (18%)
  waiting for transfers between devices  17.7 us (12%)
  Pallas kernels  16.1 us (11%)
  local copies, waits for them, and re-layouts  3.28 us (2%)
    all_to_all x1, blocking collectives, on_device(): recv = lax.all_to_all(send, VTX, 0, 0, tiled=True)  51 us
    all_to_all x1, starting transfers between devices, on_device(): want = lax.all_to_all(need, VTX, 0, 0, tiled=True)  11.9 us
    all_to_all x1, blocking collectives, on_device(): lax.all_to_all(part.reshape(n_scatter, share, LANES), SCATTER, 0, 0, tile...  11.3 us
    all_to_all x1, blocking collectives, on_device(): lax.all_to_all(part, SCATTER, 0, 0, tiled=True).reshape(half_rows, LANES)  10.1 us
    all_to_all x1, blocking collectives, on_device(): part = lax.all_to_all(part, ROUND, 0, 0, tiled=True)  9.88 us
    all_to_all x1, waiting for transfers between devices, on_device(): lax.all_to_all(aggregated.reshape(n_snap, steps_dev, rows, width), SNAP,...  9.01 us
    all_to_all x1, starting transfers between devices, on_device(): lax.all_to_all(aggregated.reshape(n_snap, steps_dev, rows, width), SNAP,...  8.69 us
    pallas_call x1, Pallas kernels, on_device(): pl.pallas_call(recur, out_shape=(jax.ShapeDtypeStruct((steps, rows, hid),...  7.98 us
  transfers between devices with their start and end apart: 4, of which 3 were waited for; matrix products, arithmetic and copies ran while one was open for 1% of the time, Pallas kernels for 0%

profile of v5, /device:TPU:1, one launch (start us, length us, event | category | flops | bytes accessed | tf_op | source)
XLA Modules:
  0.0 145.8 jit_solution(15386439043785416746)
XLA Ops:
  0.6 0.0 copy-start.2
  0.6 0.7 copy-done.2
  1.3 0.8 find_requests.1
  2.1 11.9 %all-to-all-start = ((s32[32,1,128]{2,1,0:T(1,128)}), s32[32,1,128]{2,1,0:T(1,128)S(1)}, u32[]{:S(2)}, u32[]{:S(2)}) async-start(s32[32,1,128]{2,1,0:T(1,128)} %bitcast.2), calls=%async_computation | async-start | bytes 32768 | tf_op jit(solution)/shard_map/requests/all_to_all | solution.py:276
  14.0 0.0 copy-start.1
  14.0 1.0 copy-done.1
  15.1 7.4 %all-to-all-done = s32[32,1,128]{2,1,0:T(1,128)S(1)} async-done(((s32[32,1,128]{2,1,0:T(1,128)}), s32[32,1,128]{2,1,0:T(1,128)S(1)}, u32[]{:S(2)}, u32[]{:S(2)}) %all-to-all-start) | async-done | bytes 16416 | tf_op jit(solution)/shard_map/requests/all_to_all | solution.py:276
  22.5 0.0 copy-start
  22.5 1.0 pack_blocks.1
  23.5 0.0 copy-start.3
  23.5 0.0 copy-start.6
  23.6 51.0 %all_to_all.36.recv_ref = bf16[32,2,128,128]{3,2,1,0:T(8,128)(2,1)S(1)} all-to-all(bf16[32,2,128,128]{3,2,1,0:T(8,128)(2,1)S(1)} %pack_blocks.1), channel_id=1, replica_groups=mesh['y'=4,'core'=2,'z'=8,'x'=4] {'z','x'}, dimensions={0} | all-to-all | bytes 4194304 | tf_op jit(solution)/shard_map/feature_blocks/all_to_all | solution.py:287
  74.5 0.0 copy-done
  74.5 0.0 copy-done.3
  74.6 0.0 copy-done.6
  74.6 0.0 copy-start.8
  74.6 5.2 %aggregate.1 = bf16[8,2,128,128]{3,2,1,0:T(8,128)(2,1)} custom-call(s32[2,8,16]{2,1,0:T(8,128)S(1)} %copy-done.3, s32[2,8]{1,0:T(2,128)S(1)} %copy-done.6, bf16[32,2,128,128]{3,2,1,0:T(8,128)(2,1)S(1)} %all_to_all.36.recv_ref, bf16[2,8,16,128,128]{4,3,2,1,0:T(8,128)(2,1)S(1)} %copy-done), custom_call_target="tpu_custom_call" | custom-call | tf_op jit(solution)/shard_map/aggregate/aggregate/pallas_call | solution.py:290
  79.8 0.0 copy-start.10
  79.8 0.0 copy-start.9
  79.8 0.0 copy-start.4
  79.8 0.0 copy-start.5
  79.8 0.0 copy-start.7
  79.8 8.7 %all-to-all-start.2 = ((bf16[8,2,128,128]{3,2,1,0:T(8,128)(2,1)}), bf16[8,2,128,128]{3,2,1,0:T(8,128)(2,1)S(1)}, u32[]{:S(2)}, u32[]{:S(2)}) async-start(bf16[8,2,128,128]{3,2,1,0:T(8,128)(2,1)} %aggregate.1), calls=%async_computation.2 | async-start | bytes 1048576 | tf_op jit(solution)/shard_map/to_vertices/all_to_all | solution.py:300
  88.5 0.0 copy-done.8
  88.5 0.1 copy.26
  88.7 0.0 copy-done.10
  88.7 0.1 copy.22
  88.8 0.0 copy-done.9
  88.8 0.1 copy.23
  89.0 9.0 %all-to-all-done.2 = bf16[8,2,128,128]{3,2,1,0:T(8,128)(2,1)S(1)} async-done(((bf16[8,2,128,128]{3,2,1,0:T(8,128)(2,1)}), bf16[8,2,128,128]{3,2,1,0:T(8,128)(2,1)S(1)}, u32[]{:S(2)}, u32[]{:S(2)}) %all-to-all-start.2) | async-done | bytes 524320 | tf_op jit(solution)/shard_map/to_vertices/all_to_all | solution.py:300
  98.0 0.0 copy-done.4
  98.0 0.0 copy-done.5
  98.0 0.0 copy-done.7
  98.0 8.0 %recurrence.1 = (bf16[16,128,128]{2,1,0:T(8,128)(2,1)S(1)}, f32[640,128]{1,0:T(8,128)S(1)}, f32[640,128]{1,0:T(8,128)S(1)}) custom-call(s32[1]{0:T(128)} %bitcast.core_ref, bf16[16,128,128]{2,1,0:T(8,128)(2,1)S(1)} %bitcast.23, bf16[16,128,128]{2,1,0:T(8,128)(2,1)S(1)} %bitcast.24, bf16[128,128]{1,0:T(8,128)(2,1)S(1)} %copy-done.4, f32[1,128]{1,0:T(1,128)S(1)} %bitcast.32, ...), custom_call_target="tpu_custom_call" | custom-call | tf_op jit(solution)/shard_map/recurrence/recurrence/pallas_call | solution.py:305
  106.0 1.0 collective-permute-start
  107.0 1.3 collective-permute-done.right_ref
  108.2 0.1 sum_pair.1
  108.3 11.3 %all_to_all.37.part_ref = bf16[16,40,128]{2,1,0:T(8,128)(2,1)S(1)} all-to-all(bf16[16,40,128]{2,1,0:T(8,128)(2,1)S(1)} %bitcast.27), channel_id=1, replica_groups=mesh['y'=4,'core'=2,'z'=8,'x'=4] {'x','y'}, dimensions={0} | all-to-all | bytes 327680 | tf_op jit(solution)/shard_map/gradient_sums/all_to_all | solution.py:347
  119.6 9.9 %all_to_all.38.part_ref = bf16[8,40,128]{2,1,0:T(8,128)(2,1)S(1)} all-to-all(bf16[8,40,128]{2,1,0:T(8,128)(2,1)S(1)} %sum_scattered.1), channel_id=1, replica_groups=mesh['y'=4,'core'=2,'z'=8,'x'=4] {'z'}, dimensions={0} | all-to-all | bytes 163840 | tf_op jit(solution)/shard_map/gradient_sums/all_to_all | solution.py:358
  129.6 10.1 %all_to_all.39 = bf16[16,40,128]{2,1,0:T(8,128)(2,1)S(1)} all-to-all(bf16[16,40,128]{2,1,0:T(8,128)(2,1)S(1)} %sum_round.1), channel_id=1, replica_groups=mesh['y'=4,'core'=2,'z'=8,'x'=4] {'x','y'}, dimensions={0} | all-to-all | bytes 327680 | tf_op jit(solution)/shard_map/gradient_sums/all_to_all | solution.py:367
  139.7 4.1 %collective-permute-start.1 = (bf16[640,128]{1,0:T(8,128)(2,1)S(1)}, bf16[640,128]{1,0:T(8,128)(2,1)S(1)}, u32[]{:S(2)}, u32[]{:S(2)}) collective-permute-start(bf16[640,128]{1,0:T(8,128)(2,1)S(1)} %bitcast.25), channel_id=1, source_target_pairs={{0,32},{32,0},{1,33},{33,1},{2,34},{34,2},{3,35},{35,3},{4,36},{36... | collective-permute-start | bytes 491528 | tf_op jit(solution)/shard_map/gradient_sums/ppermute | solution.py:368
  143.8 1.1 copy.24
  144.9 0.0 collective-permute-done.1.other_ref
  144.9 0.9 unpack.1
  (5 shorter events, 0.1 us)
Async XLA Ops:
  0.6 0.7 copy-start.2
  2.1 20.4 %all-to-all-start = ((s32[32,1,128]{2,1,0:T(1,128)}), s32[32,1,128]{2,1,0:T(1,128)S(1)}, u32[]{:S(2)}, u32[]{:S(2)}) async-start(s32[32,1,128]{2,1,0:T(1,128)} %bitcast.2), calls=%async_computation | async-start | bytes 32768 | tf_op jit(solution)/shard_map/requests/all_to_all | solution.py:276
  14.0 1.0 copy-start.1
  22.5 52.0 %copy-start = (bf16[2,8,16,128,128]{4,3,2,1,0:T(8,128)(2,1)S(1)}, bf16[2,8,16,128,128]{4,3,2,1,0:T(8,128)(2,1)}, u32[]{:S(2)}) copy-start(bf16[2,8,16,128,128]{4,3,2,1,0:T(8,128)(2,1)} %tile_ref.3) | copy-start | bytes 25165828
  23.5 51.0 %copy-start.3 = (s32[2,8,16]{2,1,0:T(8,128)S(1)}, s32[2,8,16]{2,1,0:T(8,128)}, u32[]{:S(2)}) copy-start(s32[2,8,16]{2,1,0:T(8,128)} %cols_ref.3) | copy-start | bytes 3076
  23.5 51.0 %copy-start.6 = (s32[2,8]{1,0:T(2,128)S(1)}, s32[2,8]{1,0:T(2,128)}, u32[]{:S(2)}) copy-start(s32[2,8]{1,0:T(2,128)} %count_ref.1) | copy-start | bytes 196
  74.6 14.0 %copy-start.8 = (bf16[1,128,16,128]{3,2,1,0:T(8,128)(2,1)S(1)}, bf16[1,128,16,128]{3,2,1,0:T(8,128)(2,1)}, u32[]{:S(2)}) copy-start(bf16[1,128,16,128]{3,2,1,0:T(8,128)(2,1)} %param.19) | copy-start | bytes 1572868
  79.8 8.9 %copy-start.10 = (bf16[128,512]{1,0:T(8,128)(2,1)S(1)}, bf16[128,512]{1,0:T(8,128)(2,1)}, u32[]{:S(2)}) copy-start(bf16[128,512]{1,0:T(8,128)(2,1)} %param.16) | copy-start | bytes 393220
  79.8 9.0 %copy-start.9 = (bf16[128,512]{1,0:T(8,128)(2,1)S(1)}, bf16[128,512]{1,0:T(8,128)(2,1)}, u32[]{:S(2)}) copy-start(bf16[128,512]{1,0:T(8,128)(2,1)} %param.17) | copy-start | bytes 393220
  79.8 18.2 %copy-start.4 = (bf16[128,128]{1,0:T(8,128)(2,1)S(1)}, bf16[128,128]{1,0:T(8,128)(2,1)}, u32[]{:S(2)}) copy-start(bf16[128,128]{1,0:T(8,128)(2,1)} %gcn_w_ref.1) | copy-start | bytes 98308
  79.8 18.2 %copy-start.5 = (f32[512]{0:T(512)S(1)}, f32[512]{0:T(512)}, u32[]{:S(2)}) copy-start(f32[512]{0:T(512)} %param.18) | copy-start | bytes 6148
  79.8 18.2 %copy-start.7 = (f32[128]{0:T(128)S(1)}, f32[128]{0:T(128)}, u32[]{:S(2)}) copy-start(f32[128]{0:T(128)} %param.15) | copy-start | bytes 1540
  79.8 18.2 %all-to-all-start.2 = ((bf16[8,2,128,128]{3,2,1,0:T(8,128)(2,1)}), bf16[8,2,128,128]{3,2,1,0:T(8,128)(2,1)S(1)}, u32[]{:S(2)}, u32[]{:S(2)}) async-start(bf16[8,2,128,128]{3,2,1,0:T(8,128)(2,1)} %aggregate.1), calls=%async_computation.2 | async-start | bytes 1048576 | tf_op jit(solution)/shard_map/to_vertices/all_to_all | solution.py:300
  106.0 2.2 %collective-permute-start = (f32[640,128]{1,0:T(8,128)S(1)}, f32[640,128]{1,0:T(8,128)S(1)}, u32[]{:S(2)}, u32[]{:S(2)}) collective-permute-start(f32[640,128]{1,0:T(8,128)S(1)} %get-tuple-element.16), channel_id=1, source_target_pairs={{0,32},{32,0},{1,33},{33,1},{2,34},{34,2},{3,35},{35,3},{4,36},{36... | collective-permute-start | bytes 983048 | tf_op jit(solution)/shard_map/gradient_sums/ppermute | solution.py:346
  139.7 5.2 %collective-permute-start.1 = (bf16[640,128]{1,0:T(8,128)(2,1)S(1)}, bf16[640,128]{1,0:T(8,128)(2,1)S(1)}, u32[]{:S(2)}, u32[]{:S(2)}) collective-permute-start(bf16[640,128]{1,0:T(8,128)(2,1)S(1)} %bitcast.25), channel_id=1, source_target_pairs={{0,32},{32,0},{1,33},{33,1},{2,34},{34,2},{3,35},{35,3},{4,36},{36... | collective-permute-start | bytes 491528 | tf_op jit(solution)/shard_map/gradient_sums/ppermute | solution.py:368

commit v6 on v5

--- a/solution.py
+++ b/solution.py
@@ -68,30 +68,35 @@
             send_ref[peer, step] = feat_ref[step, pick]
         return 0
 
-    lax.fori_loop(0, peers, fill, 0, unroll=4)
+    lax.fori_loop(0, peers, fill, 0, unroll=8)
 
 
 def aggregate(cols_ref, count_ref, recv_ref, tile_ref, out_ref, *, per_peer):
     steps, blocks, slots, size = tile_ref.shape[:4]
     peers, width = recv_ref.shape[0], recv_ref.shape[3]
 
-    def one_block(block, _):
+    def add_up(block, lives, taken):
         for step in range(steps):
-            live = count_ref[step, block]
             total = jnp.zeros((size, width), F32)
-            for slot in range(0, slots, 2):
+            for slot in range(0, taken, 2):
                 tiles, held = [], []
                 for at in (slot, slot + 1):
                     peer = jnp.clip(lax.div(cols_ref[step, block, at], per_peer), 0, peers - 1)
                     picked = recv_ref[peer, step]
                     tiles.append(tile_ref[step, block, at])
-                    held.append(lax.select_n(at < live, jnp.zeros_like(picked), picked))
+                    held.append(lax.select_n(at < lives[step], jnp.zeros_like(picked), picked))
                 total = total + jnp.dot(
                     jnp.concatenate(tiles, axis=1),
                     jnp.concatenate(held, axis=0),
                     preferred_element_type=F32,
                 )
             out_ref[block, step] = total.astype(BF16)
+
+    def one_block(block, _):
+        lives = [count_ref[step, block] for step in range(steps)]
+        few = functools.reduce(jnp.maximum, lives) <= slots // 2
+        pl.when(few)(lambda: add_up(block, lives, slots // 2))
+        pl.when(jnp.logical_not(few))(lambda: add_up(block, lives, slots))
         return 0
 
     lax.fori_loop(0, blocks, one_block, 0)
@@ -154,7 +159,7 @@
         out_ref[t] = out
         return 0
 
-    lax.fori_loop(0, steps, advance, 0, unroll=4)
+    lax.fori_loop(0, steps, advance, 0, unroll=8)
 
     def retreat(k, carried):
         grad_cell, grad_back = carried
@@ -182,7 +187,7 @@
         return grad_cell * gate_keep, back[:, width:]
 
     zero = jnp.zeros((rows, hid), F32)
-    lax.fori_loop(0, steps, retreat, (zero, zero), unroll=4)
+    lax.fori_loop(0, steps, retreat, (zero, zero), unroll=8)
 
     flat_dgates = dgates_s[...].reshape(steps * rows, 4 * hid)
     flat_dpre = dpre_s[...].reshape(steps * rows, width)

time: 146 us -> 146 us (level)
  no operation moved by 1% of the time
where the time goes in v6:
time: 146 us; the launch traced here: 145 us
  blocking collectives  82.4 us (56%)
  starting transfers between devices  25.8 us (18%)
  waiting for transfers between devices  17.7 us (12%)
  Pallas kernels  15.5 us (11%)
  local copies, waits for them, and re-layouts  3.28 us (2%)
    all_to_all x1, blocking collectives, on_device(): recv = lax.all_to_all(send, VTX, 0, 0, tiled=True)  51 us
    all_to_all x1, starting transfers between devices, on_device(): want = lax.all_to_all(need, VTX, 0, 0, tiled=True)  11.9 us
    all_to_all x1, blocking collectives, on_device(): lax.all_to_all(part.reshape(n_scatter, share, LANES), SCATTER, 0, 0, tile...  11.4 us
    all_to_all x1, blocking collectives, on_device(): lax.all_to_all(part, SCATTER, 0, 0, tiled=True).reshape(half_rows, LANES)  10.1 us
    all_to_all x1, blocking collectives, on_device(): part = lax.all_to_all(part, ROUND, 0, 0, tiled=True)  9.88 us
    all_to_all x1, waiting for transfers between devices, on_device(): lax.all_to_all(aggregated.reshape(n_snap, steps_dev, rows, width), SNAP,...  9.01 us
    all_to_all x1, starting transfers between devices, on_device(): lax.all_to_all(aggregated.reshape(n_snap, steps_dev, rows, width), SNAP,...  8.85 us
    pallas_call x1, Pallas kernels, on_device(): pl.pallas_call(recur, out_shape=(jax.ShapeDtypeStruct((steps, rows, hid),...  7.77 us
  transfers between devices with their start and end apart: 4, of which 3 were waited for; matrix products, arithmetic and copies ran while one was open for 1% of the time, Pallas kernels for 0%

profile of v6, /device:TPU:1, one launch (start us, length us, event | category | flops | bytes accessed | tf_op | source)
XLA Modules:
  0.0 145.4 jit_solution(631974133362067243)
XLA Ops:
  0.6 0.0 copy-start.2
  0.6 0.7 copy-done.2
  1.3 0.8 find_requests.1
  2.1 11.9 %all-to-all-start = ((s32[32,1,128]{2,1,0:T(1,128)}), s32[32,1,128]{2,1,0:T(1,128)S(1)}, u32[]{:S(2)}, u32[]{:S(2)}) async-start(s32[32,1,128]{2,1,0:T(1,128)} %bitcast.2), calls=%async_computation | async-start | bytes 32768 | tf_op jit(solution)/shard_map/requests/all_to_all | solution.py:281
  14.0 0.0 copy-start.1
  14.0 1.0 copy-done.1
  15.1 7.4 %all-to-all-done = s32[32,1,128]{2,1,0:T(1,128)S(1)} async-done(((s32[32,1,128]{2,1,0:T(1,128)}), s32[32,1,128]{2,1,0:T(1,128)S(1)}, u32[]{:S(2)}, u32[]{:S(2)}) %all-to-all-start) | async-done | bytes 16416 | tf_op jit(solution)/shard_map/requests/all_to_all | solution.py:281
  22.5 0.0 copy-start
  22.5 1.0 pack_blocks.1
  23.5 0.0 copy-start.3
  23.5 0.0 copy-start.6
  23.5 51.0 %all_to_all.36.recv_ref = bf16[32,2,128,128]{3,2,1,0:T(8,128)(2,1)S(1)} all-to-all(bf16[32,2,128,128]{3,2,1,0:T(8,128)(2,1)S(1)} %pack_blocks.1), channel_id=1, replica_groups=mesh['y'=4,'core'=2,'z'=8,'x'=4] {'z','x'}, dimensions={0} | all-to-all | bytes 4194304 | tf_op jit(solution)/shard_map/feature_blocks/all_to_all | solution.py:292
  74.5 0.0 copy-done
  74.5 0.0 copy-done.3
  74.5 0.0 copy-done.6
  74.5 0.0 copy-start.8
  74.5 4.9 %aggregate.1 = bf16[8,2,128,128]{3,2,1,0:T(8,128)(2,1)} custom-call(s32[2,8,16]{2,1,0:T(8,128)S(1)} %copy-done.3, s32[2,8]{1,0:T(2,128)S(1)} %copy-done.6, bf16[32,2,128,128]{3,2,1,0:T(8,128)(2,1)S(1)} %all_to_all.36.recv_ref, bf16[2,8,16,128,128]{4,3,2,1,0:T(8,128)(2,1)S(1)} %copy-done), custom_call_target="tpu_custom_call" | custom-call | tf_op jit(solution)/shard_map/aggregate/aggregate/pallas_call | solution.py:295
  79.4 0.0 copy-start.10
  79.4 0.0 copy-start.9
  79.4 0.0 copy-start.4
  79.4 0.0 copy-start.5
  79.4 0.0 copy-start.7
  79.4 8.8 %all-to-all-start.2 = ((bf16[8,2,128,128]{3,2,1,0:T(8,128)(2,1)}), bf16[8,2,128,128]{3,2,1,0:T(8,128)(2,1)S(1)}, u32[]{:S(2)}, u32[]{:S(2)}) async-start(bf16[8,2,128,128]{3,2,1,0:T(8,128)(2,1)} %aggregate.1), calls=%async_computation.2 | async-start | bytes 1048576 | tf_op jit(solution)/shard_map/to_vertices/all_to_all | solution.py:305
  88.3 0.0 copy-done.8
  88.3 0.1 copy.26
  88.4 0.0 copy-done.10
  88.4 0.1 copy.22
  88.6 0.0 copy-done.9
  88.6 0.1 copy.23
  88.8 9.0 %all-to-all-done.2 = bf16[8,2,128,128]{3,2,1,0:T(8,128)(2,1)S(1)} async-done(((bf16[8,2,128,128]{3,2,1,0:T(8,128)(2,1)}), bf16[8,2,128,128]{3,2,1,0:T(8,128)(2,1)S(1)}, u32[]{:S(2)}, u32[]{:S(2)}) %all-to-all-start.2) | async-done | bytes 524320 | tf_op jit(solution)/shard_map/to_vertices/all_to_all | solution.py:305
  97.8 0.0 copy-done.4
  97.8 0.0 copy-done.5
  97.8 0.0 copy-done.7
  97.8 7.8 %recurrence.1 = (bf16[16,128,128]{2,1,0:T(8,128)(2,1)S(1)}, f32[640,128]{1,0:T(8,128)S(1)}, f32[640,128]{1,0:T(8,128)S(1)}) custom-call(s32[1]{0:T(128)} %bitcast.core_ref, bf16[16,128,128]{2,1,0:T(8,128)(2,1)S(1)} %bitcast.23, bf16[16,128,128]{2,1,0:T(8,128)(2,1)S(1)} %bitcast.24, bf16[128,128]{1,0:T(8,128)(2,1)S(1)} %copy-done.4, f32[1,128]{1,0:T(1,128)S(1)} %bitcast.32, ...), custom_call_target="tpu_custom_call" | custom-call | tf_op jit(solution)/shard_map/recurrence/recurrence/pallas_call | solution.py:310
  105.5 1.0 collective-permute-start
  106.5 1.3 collective-permute-done.right_ref
  107.8 0.1 sum_pair.1
  107.8 11.4 %all_to_all.37.part_ref = bf16[16,40,128]{2,1,0:T(8,128)(2,1)S(1)} all-to-all(bf16[16,40,128]{2,1,0:T(8,128)(2,1)S(1)} %bitcast.27), channel_id=1, replica_groups=mesh['y'=4,'core'=2,'z'=8,'x'=4] {'x','y'}, dimensions={0} | all-to-all | bytes 327680 | tf_op jit(solution)/shard_map/gradient_sums/all_to_all | solution.py:352
  119.3 9.9 %all_to_all.38.part_ref = bf16[8,40,128]{2,1,0:T(8,128)(2,1)S(1)} all-to-all(bf16[8,40,128]{2,1,0:T(8,128)(2,1)S(1)} %sum_scattered.1), channel_id=1, replica_groups=mesh['y'=4,'core'=2,'z'=8,'x'=4] {'z'}, dimensions={0} | all-to-all | bytes 163840 | tf_op jit(solution)/shard_map/gradient_sums/all_to_all | solution.py:363
  129.2 10.1 %all_to_all.39 = bf16[16,40,128]{2,1,0:T(8,128)(2,1)S(1)} all-to-all(bf16[16,40,128]{2,1,0:T(8,128)(2,1)S(1)} %sum_round.1), channel_id=1, replica_groups=mesh['y'=4,'core'=2,'z'=8,'x'=4] {'x','y'}, dimensions={0} | all-to-all | bytes 327680 | tf_op jit(solution)/shard_map/gradient_sums/all_to_all | solution.py:372
  139.3 4.1 %collective-permute-start.1 = (bf16[640,128]{1,0:T(8,128)(2,1)S(1)}, bf16[640,128]{1,0:T(8,128)(2,1)S(1)}, u32[]{:S(2)}, u32[]{:S(2)}) collective-permute-start(bf16[640,128]{1,0:T(8,128)(2,1)S(1)} %bitcast.25), channel_id=1, source_target_pairs={{0,32},{32,0},{1,33},{33,1},{2,34},{34,2},{3,35},{35,3},{4,36},{36... | collective-permute-start | bytes 491528 | tf_op jit(solution)/shard_map/gradient_sums/ppermute | solution.py:373
  143.4 1.1 copy.24
  144.5 0.0 collective-permute-done.1.other_ref
  144.6 0.9 unpack.1
  (5 shorter events, 0.1 us)
Async XLA Ops:
  0.6 0.7 copy-start.2
  2.1 20.4 %all-to-all-start = ((s32[32,1,128]{2,1,0:T(1,128)}), s32[32,1,128]{2,1,0:T(1,128)S(1)}, u32[]{:S(2)}, u32[]{:S(2)}) async-start(s32[32,1,128]{2,1,0:T(1,128)} %bitcast.2), calls=%async_computation | async-start | bytes 32768 | tf_op jit(solution)/shard_map/requests/all_to_all | solution.py:281
  14.0 1.0 copy-start.1
  22.5 52.0 %copy-start = (bf16[2,8,16,128,128]{4,3,2,1,0:T(8,128)(2,1)S(1)}, bf16[2,8,16,128,128]{4,3,2,1,0:T(8,128)(2,1)}, u32[]{:S(2)}) copy-start(bf16[2,8,16,128,128]{4,3,2,1,0:T(8,128)(2,1)} %tile_ref.3) | copy-start | bytes 25165828
  23.5 51.0 %copy-start.3 = (s32[2,8,16]{2,1,0:T(8,128)S(1)}, s32[2,8,16]{2,1,0:T(8,128)}, u32[]{:S(2)}) copy-start(s32[2,8,16]{2,1,0:T(8,128)} %cols_ref.3) | copy-start | bytes 3076
  23.5 51.0 %copy-start.6 = (s32[2,8]{1,0:T(2,128)S(1)}, s32[2,8]{1,0:T(2,128)}, u32[]{:S(2)}) copy-start(s32[2,8]{1,0:T(2,128)} %count_ref.1) | copy-start | bytes 196
  74.5 13.8 %copy-start.8 = (bf16[1,128,16,128]{3,2,1,0:T(8,128)(2,1)S(1)}, bf16[1,128,16,128]{3,2,1,0:T(8,128)(2,1)}, u32[]{:S(2)}) copy-start(bf16[1,128,16,128]{3,2,1,0:T(8,128)(2,1)} %param.19) | copy-start | bytes 1572868
  79.4 9.0 %copy-start.10 = (bf16[128,512]{1,0:T(8,128)(2,1)S(1)}, bf16[128,512]{1,0:T(8,128)(2,1)}, u32[]{:S(2)}) copy-start(bf16[128,512]{1,0:T(8,128)(2,1)} %param.16) | copy-start | bytes 393220
  79.4 9.1 %copy-start.9 = (bf16[128,512]{1,0:T(8,128)(2,1)S(1)}, bf16[128,512]{1,0:T(8,128)(2,1)}, u32[]{:S(2)}) copy-start(bf16[128,512]{1,0:T(8,128)(2,1)} %param.17) | copy-start | bytes 393220
  79.4 18.4 %copy-start.4 = (bf16[128,128]{1,0:T(8,128)(2,1)S(1)}, bf16[128,128]{1,0:T(8,128)(2,1)}, u32[]{:S(2)}) copy-start(bf16[128,128]{1,0:T(8,128)(2,1)} %gcn_w_ref.1) | copy-start | bytes 98308
  79.4 18.4 %copy-start.5 = (f32[512]{0:T(512)S(1)}, f32[512]{0:T(512)}, u32[]{:S(2)}) copy-start(f32[512]{0:T(512)} %param.18) | copy-start | bytes 6148
  79.4 18.3 %copy-start.7 = (f32[128]{0:T(128)S(1)}, f32[128]{0:T(128)}, u32[]{:S(2)}) copy-start(f32[128]{0:T(128)} %param.15) | copy-start | bytes 1540
  79.4 18.3 %all-to-all-start.2 = ((bf16[8,2,128,128]{3,2,1,0:T(8,128)(2,1)}), bf16[8,2,128,128]{3,2,1,0:T(8,128)(2,1)S(1)}, u32[]{:S(2)}, u32[]{:S(2)}) async-start(bf16[8,2,128,128]{3,2,1,0:T(8,128)(2,1)} %aggregate.1), calls=%async_computation.2 | async-start | bytes 1048576 | tf_op jit(solution)/shard_map/to_vertices/all_to_all | solution.py:305
  105.5 2.2 %collective-permute-start = (f32[640,128]{1,0:T(8,128)S(1)}, f32[640,128]{1,0:T(8,128)S(1)}, u32[]{:S(2)}, u32[]{:S(2)}) collective-permute-start(f32[640,128]{1,0:T(8,128)S(1)} %get-tuple-element.16), channel_id=1, source_target_pairs={{0,32},{32,0},{1,33},{33,1},{2,34},{34,2},{3,35},{35,3},{4,36},{36... | collective-permute-start | bytes 983048 | tf_op jit(solution)/shard_map/gradient_sums/ppermute | solution.py:351
  139.3 5.2 %collective-permute-start.1 = (bf16[640,128]{1,0:T(8,128)(2,1)S(1)}, bf16[640,128]{1,0:T(8,128)(2,1)S(1)}, u32[]{:S(2)}, u32[]{:S(2)}) collective-permute-start(bf16[640,128]{1,0:T(8,128)(2,1)S(1)} %bitcast.25), channel_id=1, source_target_pairs={{0,32},{32,0},{1,33},{33,1},{2,34},{34,2},{3,35},{35,3},{4,36},{36... | collective-permute-start | bytes 491528 | tf_op jit(solution)/shard_map/gradient_sums/ppermute | solution.py:373

commit v7 on v6

--- a/solution.py
+++ b/solution.py
@@ -134,7 +134,7 @@
         slope_s[t] = squeeze * (1.0 + pre * (1.0 - squeeze))
         return 0
 
-    lax.fori_loop(0, steps, layer, 0, unroll=4)
+    lax.fori_loop(0, steps, layer, 0, unroll=8)
 
     hprev_s[0] = jnp.zeros((rows, hid), BF16)
     cell_s[0] = jnp.zeros((rows, hid), F32)

time: 146 us -> 145 us (level)
  no operation moved by 1% of the time
where the time goes in v7:
time: 145 us
  blocking collectives  82.3 us (57%)
  starting transfers between devices  25.7 us (18%)
  waiting for transfers between devices  17.7 us (12%)
  Pallas kernels  15 us (10%)
  local copies, waits for them, and re-layouts  3.28 us (2%)
    all_to_all x1, blocking collectives, on_device(): recv = lax.all_to_all(send, VTX, 0, 0, tiled=True)  51 us
    all_to_all x1, starting transfers between devices, on_device(): want = lax.all_to_all(need, VTX, 0, 0, tiled=True)  11.9 us
    all_to_all x1, blocking collectives, on_device(): lax.all_to_all(part.reshape(n_scatter, share, LANES), SCATTER, 0, 0, tile...  11.3 us
    all_to_all x1, blocking collectives, on_device(): lax.all_to_all(part, SCATTER, 0, 0, tiled=True).reshape(half_rows, LANES)  10.1 us
    all_to_all x1, blocking collectives, on_device(): part = lax.all_to_all(part, ROUND, 0, 0, tiled=True)  9.88 us
    all_to_all x1, waiting for transfers between devices, on_device(): lax.all_to_all(aggregated.reshape(n_snap, steps_dev, rows, width), SNAP,...  9.01 us
    all_to_all x1, starting transfers between devices, on_device(): lax.all_to_all(aggregated.reshape(n_snap, steps_dev, rows, width), SNAP,...  8.84 us
    pallas_call x1, Pallas kernels, on_device(): pl.pallas_call(recur, out_shape=(jax.ShapeDtypeStruct((steps, rows, hid),...  7.49 us
  transfers between devices with their start and end apart: 4, of which 3 were waited for; matrix products, arithmetic and copies ran while one was open for 1% of the time, Pallas kernels for 0%

profile of v7, /device:TPU:1, one launch (start us, length us, event | category | flops | bytes accessed | tf_op | source)
XLA Modules:
  0.0 144.9 jit_solution(7913322390568865387)
XLA Ops:
  0.6 0.0 copy-start.2
  0.6 0.7 copy-done.2
  1.3 0.8 find_requests.1
  2.1 11.9 %all-to-all-start = ((s32[32,1,128]{2,1,0:T(1,128)}), s32[32,1,128]{2,1,0:T(1,128)S(1)}, u32[]{:S(2)}, u32[]{:S(2)}) async-start(s32[32,1,128]{2,1,0:T(1,128)} %bitcast.2), calls=%async_computation | async-start | bytes 32768 | tf_op jit(solution)/shard_map/requests/all_to_all | solution.py:281
  14.0 0.0 copy-start.1
  14.0 1.0 copy-done.1
  15.1 7.4 %all-to-all-done = s32[32,1,128]{2,1,0:T(1,128)S(1)} async-done(((s32[32,1,128]{2,1,0:T(1,128)}), s32[32,1,128]{2,1,0:T(1,128)S(1)}, u32[]{:S(2)}, u32[]{:S(2)}) %all-to-all-start) | async-done | bytes 16416 | tf_op jit(solution)/shard_map/requests/all_to_all | solution.py:281
  22.5 0.0 copy-start
  22.5 1.0 pack_blocks.1
  23.5 0.0 copy-start.3
  23.5 0.0 copy-start.6
  23.5 51.0 %all_to_all.36.recv_ref = bf16[32,2,128,128]{3,2,1,0:T(8,128)(2,1)S(1)} all-to-all(bf16[32,2,128,128]{3,2,1,0:T(8,128)(2,1)S(1)} %pack_blocks.1), channel_id=1, replica_groups=mesh['y'=4,'core'=2,'z'=8,'x'=4] {'z','x'}, dimensions={0} | all-to-all | bytes 4194304 | tf_op jit(solution)/shard_map/feature_blocks/all_to_all | solution.py:292
  74.5 0.0 copy-done
  74.5 0.0 copy-done.3
  74.5 0.0 copy-done.6
  74.5 0.0 copy-start.8
  74.5 4.7 %aggregate.1 = bf16[8,2,128,128]{3,2,1,0:T(8,128)(2,1)} custom-call(s32[2,8,16]{2,1,0:T(8,128)S(1)} %copy-done.3, s32[2,8]{1,0:T(2,128)S(1)} %copy-done.6, bf16[32,2,128,128]{3,2,1,0:T(8,128)(2,1)S(1)} %all_to_all.36.recv_ref, bf16[2,8,16,128,128]{4,3,2,1,0:T(8,128)(2,1)S(1)} %copy-done), custom_call_target="tpu_custom_call" | custom-call | tf_op jit(solution)/shard_map/aggregate/aggregate/pallas_call | solution.py:295
  79.3 0.0 copy-start.10
  79.3 0.0 copy-start.9
  79.3 0.0 copy-start.4
  79.3 0.0 copy-start.5
  79.3 0.0 copy-start.7
  79.3 8.8 %all-to-all-start.2 = ((bf16[8,2,128,128]{3,2,1,0:T(8,128)(2,1)}), bf16[8,2,128,128]{3,2,1,0:T(8,128)(2,1)S(1)}, u32[]{:S(2)}, u32[]{:S(2)}) async-start(bf16[8,2,128,128]{3,2,1,0:T(8,128)(2,1)} %aggregate.1), calls=%async_computation.2 | async-start | bytes 1048576 | tf_op jit(solution)/shard_map/to_vertices/all_to_all | solution.py:305
  88.1 0.0 copy-done.8
  88.1 0.1 copy.26
  88.3 0.0 copy-done.10
  88.3 0.1 copy.22
  88.4 0.0 copy-done.9
  88.4 0.1 copy.23
  88.6 9.0 %all-to-all-done.2 = bf16[8,2,128,128]{3,2,1,0:T(8,128)(2,1)S(1)} async-done(((bf16[8,2,128,128]{3,2,1,0:T(8,128)(2,1)}), bf16[8,2,128,128]{3,2,1,0:T(8,128)(2,1)S(1)}, u32[]{:S(2)}, u32[]{:S(2)}) %all-to-all-start.2) | async-done | bytes 524320 | tf_op jit(solution)/shard_map/to_vertices/all_to_all | solution.py:305
  97.6 0.0 copy-done.4
  97.6 0.0 copy-done.5
  97.6 0.0 copy-done.7
  97.6 7.5 %recurrence.1 = (bf16[16,128,128]{2,1,0:T(8,128)(2,1)S(1)}, f32[640,128]{1,0:T(8,128)S(1)}, f32[640,128]{1,0:T(8,128)S(1)}) custom-call(s32[1]{0:T(128)} %bitcast.core_ref, bf16[16,128,128]{2,1,0:T(8,128)(2,1)S(1)} %bitcast.23, bf16[16,128,128]{2,1,0:T(8,128)(2,1)S(1)} %bitcast.24, bf16[128,128]{1,0:T(8,128)(2,1)S(1)} %copy-done.4, f32[1,128]{1,0:T(1,128)S(1)} %bitcast.32, ...), custom_call_target="tpu_custom_call" | custom-call | tf_op jit(solution)/shard_map/recurrence/recurrence/pallas_call | solution.py:310
  105.1 1.0 collective-permute-start
  106.1 1.3 collective-permute-done.right_ref
  107.3 0.1 sum_pair.1
  107.4 11.3 %all_to_all.37.part_ref = bf16[16,40,128]{2,1,0:T(8,128)(2,1)S(1)} all-to-all(bf16[16,40,128]{2,1,0:T(8,128)(2,1)S(1)} %bitcast.27), channel_id=1, replica_groups=mesh['y'=4,'core'=2,'z'=8,'x'=4] {'x','y'}, dimensions={0} | all-to-all | bytes 327680 | tf_op jit(solution)/shard_map/gradient_sums/all_to_all | solution.py:352
  118.7 9.9 %all_to_all.38.part_ref = bf16[8,40,128]{2,1,0:T(8,128)(2,1)S(1)} all-to-all(bf16[8,40,128]{2,1,0:T(8,128)(2,1)S(1)} %sum_scattered.1), channel_id=1, replica_groups=mesh['y'=4,'core'=2,'z'=8,'x'=4] {'z'}, dimensions={0} | all-to-all | bytes 163840 | tf_op jit(solution)/shard_map/gradient_sums/all_to_all | solution.py:363
  128.6 10.1 %all_to_all.39 = bf16[16,40,128]{2,1,0:T(8,128)(2,1)S(1)} all-to-all(bf16[16,40,128]{2,1,0:T(8,128)(2,1)S(1)} %sum_round.1), channel_id=1, replica_groups=mesh['y'=4,'core'=2,'z'=8,'x'=4] {'x','y'}, dimensions={0} | all-to-all | bytes 327680 | tf_op jit(solution)/shard_map/gradient_sums/all_to_all | solution.py:372
  138.8 4.1 %collective-permute-start.1 = (bf16[640,128]{1,0:T(8,128)(2,1)S(1)}, bf16[640,128]{1,0:T(8,128)(2,1)S(1)}, u32[]{:S(2)}, u32[]{:S(2)}) collective-permute-start(bf16[640,128]{1,0:T(8,128)(2,1)S(1)} %bitcast.25), channel_id=1, source_target_pairs={{0,32},{32,0},{1,33},{33,1},{2,34},{34,2},{3,35},{35,3},{4,36},{36... | collective-permute-start | bytes 491528 | tf_op jit(solution)/shard_map/gradient_sums/ppermute | solution.py:373
  142.9 1.1 copy.24
  144.0 0.0 collective-permute-done.1.other_ref
  144.0 0.9 unpack.1
  (5 shorter events, 0.1 us)
Async XLA Ops:
  0.6 0.7 copy-start.2
  2.1 20.4 %all-to-all-start = ((s32[32,1,128]{2,1,0:T(1,128)}), s32[32,1,128]{2,1,0:T(1,128)S(1)}, u32[]{:S(2)}, u32[]{:S(2)}) async-start(s32[32,1,128]{2,1,0:T(1,128)} %bitcast.2), calls=%async_computation | async-start | bytes 32768 | tf_op jit(solution)/shard_map/requests/all_to_all | solution.py:281
  14.0 1.0 copy-start.1
  22.5 52.0 %copy-start = (bf16[2,8,16,128,128]{4,3,2,1,0:T(8,128)(2,1)S(1)}, bf16[2,8,16,128,128]{4,3,2,1,0:T(8,128)(2,1)}, u32[]{:S(2)}) copy-start(bf16[2,8,16,128,128]{4,3,2,1,0:T(8,128)(2,1)} %tile_ref.3) | copy-start | bytes 25165828
  23.5 51.0 %copy-start.3 = (s32[2,8,16]{2,1,0:T(8,128)S(1)}, s32[2,8,16]{2,1,0:T(8,128)}, u32[]{:S(2)}) copy-start(s32[2,8,16]{2,1,0:T(8,128)} %cols_ref.3) | copy-start | bytes 3076
  23.5 51.0 %copy-start.6 = (s32[2,8]{1,0:T(2,128)S(1)}, s32[2,8]{1,0:T(2,128)}, u32[]{:S(2)}) copy-start(s32[2,8]{1,0:T(2,128)} %count_ref.1) | copy-start | bytes 196
  74.5 13.6 %copy-start.8 = (bf16[1,128,16,128]{3,2,1,0:T(8,128)(2,1)S(1)}, bf16[1,128,16,128]{3,2,1,0:T(8,128)(2,1)}, u32[]{:S(2)}) copy-start(bf16[1,128,16,128]{3,2,1,0:T(8,128)(2,1)} %param.19) | copy-start | bytes 1572868
  79.3 9.0 %copy-start.10 = (bf16[128,512]{1,0:T(8,128)(2,1)S(1)}, bf16[128,512]{1,0:T(8,128)(2,1)}, u32[]{:S(2)}) copy-start(bf16[128,512]{1,0:T(8,128)(2,1)} %param.16) | copy-start | bytes 393220
  79.3 9.1 %copy-start.9 = (bf16[128,512]{1,0:T(8,128)(2,1)S(1)}, bf16[128,512]{1,0:T(8,128)(2,1)}, u32[]{:S(2)}) copy-start(bf16[128,512]{1,0:T(8,128)(2,1)} %param.17) | copy-start | bytes 393220
  79.3 18.3 %copy-start.4 = (bf16[128,128]{1,0:T(8,128)(2,1)S(1)}, bf16[128,128]{1,0:T(8,128)(2,1)}, u32[]{:S(2)}) copy-start(bf16[128,128]{1,0:T(8,128)(2,1)} %gcn_w_ref.1) | copy-start | bytes 98308
  79.3 18.3 %copy-start.5 = (f32[512]{0:T(512)S(1)}, f32[512]{0:T(512)}, u32[]{:S(2)}) copy-start(f32[512]{0:T(512)} %param.18) | copy-start | bytes 6148
  79.3 18.3 %copy-start.7 = (f32[128]{0:T(128)S(1)}, f32[128]{0:T(128)}, u32[]{:S(2)}) copy-start(f32[128]{0:T(128)} %param.15) | copy-start | bytes 1540
  79.3 18.3 %all-to-all-start.2 = ((bf16[8,2,128,128]{3,2,1,0:T(8,128)(2,1)}), bf16[8,2,128,128]{3,2,1,0:T(8,128)(2,1)S(1)}, u32[]{:S(2)}, u32[]{:S(2)}) async-start(bf16[8,2,128,128]{3,2,1,0:T(8,128)(2,1)} %aggregate.1), calls=%async_computation.2 | async-start | bytes 1048576 | tf_op jit(solution)/shard_map/to_vertices/all_to_all | solution.py:305
  105.1 2.2 %collective-permute-start = (f32[640,128]{1,0:T(8,128)S(1)}, f32[640,128]{1,0:T(8,128)S(1)}, u32[]{:S(2)}, u32[]{:S(2)}) collective-permute-start(f32[640,128]{1,0:T(8,128)S(1)} %get-tuple-element.16), channel_id=1, source_target_pairs={{0,32},{32,0},{1,33},{33,1},{2,34},{34,2},{3,35},{35,3},{4,36},{36... | collective-permute-start | bytes 983048 | tf_op jit(solution)/shard_map/gradient_sums/ppermute | solution.py:351
  138.8 5.2 %collective-permute-start.1 = (bf16[640,128]{1,0:T(8,128)(2,1)S(1)}, bf16[640,128]{1,0:T(8,128)(2,1)S(1)}, u32[]{:S(2)}, u32[]{:S(2)}) collective-permute-start(bf16[640,128]{1,0:T(8,128)(2,1)S(1)} %bitcast.25), channel_id=1, source_target_pairs={{0,32},{32,0},{1,33},{33,1},{2,34},{34,2},{3,35},{35,3},{4,36},{36... | collective-permute-start | bytes 491528 | tf_op jit(solution)/shard_map/gradient_sums/ppermute | solution.py:373
